TPU v7x, 32 devices: a whole 2x2x4 slice. The times are simulated.
32 devices in a mesh: groups: 2 (over y), strip: 4 (over z), angle: 2 (over x), depth: 2 (over core).
Axes of the slice: x: 2, y: 2, z: 4, core: 2. Of those that a mesh axis runs over, the one named last changes fastest.
Arguments:
- crystal: bfloat16 [16, 2, 512, 384], P(('groups', 'depth'), None, 'strip'), parts along dimension 0, may hold values from -4 to 4
- probe: bfloat16 [2, 256, 256], replicated, may hold values from -5 to 5
- amplitude: bfloat16 [4, 2048, 256], P('angle', ('groups', 'strip', 'depth')), parts along dimension 1, may hold values from 0.5 to 8
- shear: int32 [16, 8], P(('groups', 'angle'), 'depth'), parts along dimension 0, may hold values from 0 to 15
- scan_x: int32 [4, 4, 2], P(('groups', 'angle')), parts along dimension 0, may hold values from 0 to 112
- scan_y: int32 [4, 4, 2], P(('groups', 'angle')), parts along dimension 0, may hold values from 0 to 128
- slot_angle: int32 [4, 4, 2], P(('groups', 'angle')), parts along dimension 0, may hold values from 0 to 3
- owner_slot: int32 [4, 4, 2], P(('groups', 'angle')), parts along dimension 0, may hold values from 0 to 1, each once within a row
- counts: int32 [4, 4], P(('groups', 'angle')), parts along dimension 0, may hold values from 1 to 2
Outputs:
- gradient: float32 [16, 2, 512, 384], P(('groups', 'depth'), None, ('strip', 'angle')), parts along dimension 0
There are 2 independent parts, one for each index of `groups`. A program takes and returns all parts, laid end to end along the dimension named above; an argument that names none is the same for every part. Nothing has to cross between parts.
Inputs may be any that keep to these rules, and one draw needn't show every extreme that they name: `owner_slot`: for each angle group and home strip, the 2 entries are a permutation of 0 to 1.
All inputs are finite; a program needn't handle non-finite values.
Results may differ from a plain program's by a relative error of at most 0.02.
Values may be sent and summed in bfloat16 or wider, within the bound.
A program may use at most 64 MiB of HBM per device.

v0:
```python
import functools

import jax
import jax.numpy as jnp
import numpy as np
from jax import lax
from jax.experimental import pallas as pl
from jax.experimental.pallas import tpu as pltpu
from jax.sharding import PartitionSpec as P

FRAME = 256
WX = 128
SHEAR = 16
REACHES = 3
ROWS = (WX, FRAME, FRAME - WX)
BASES = (0, 0, WX)
MESH = pl.DeviceIdType.MESH


def dft_tables():
    index_row = np.arange(FRAME)
    phase = (index_row[:, None] * index_row[None, :] % FRAME) * (2.0 * np.pi / FRAME)
    real = np.cos(phase) / np.sqrt(FRAME)
    imag = -np.sin(phase) / np.sqrt(FRAME)
    table = np.block([[real, imag], [-imag, real]]).astype(np.float32)
    return jnp.asarray(table, jnp.bfloat16), jnp.asarray(table.T, jnp.bfloat16)


def dot(left, right):
    return jnp.dot(left, right, preferred_element_type=jnp.float32)


def differences(rows, columns):
    shape = (rows, columns)
    return lax.broadcasted_iota(jnp.int32, shape, 1) - lax.broadcasted_iota(jnp.int32, shape, 0)


def one_hot(mask):
    return jnp.where(mask, 1.0, 0.0).astype(jnp.bfloat16)


class Meta:
    def __init__(self, lifts, owner_slot, slots, lead):
        self.lifts, self.owner_slot = lifts, owner_slot
        self.slots, self.lead = slots, lead

    def shear(self, angle, z):
        return self.lifts[self.lead + (angle, z)]

    def pick(self, ref, home, quota):
        value = jnp.int32(0)
        for m in range(self.slots):
            at = self.lead + (0, m, home)
            value = value + jnp.where(self.owner_slot[at] == quota, ref[at], 0)
        return value

    def slot(self, home, quota):
        value = jnp.int32(0)
        for m in range(self.slots):
            at = self.lead + (0, m, home)
            value = value + jnp.where(self.owner_slot[at] == quota, m, 0)
        return value


def kernel(
    sizes,
    crystal,
    probe_in,
    amplitude,
    table_in,
    table_t_in,
    shear,
    scan_x,
    scan_y,
    slot_angle,
    owner_slot,
    counts,
    shear_in,
    scan_y_in,
    slot_angle_in,
    owner_slot_in,
    windows,
    shear_out,
    scan_y_out,
    slot_angle_out,
    owner_slot_out,
    film,
    probe,
    table,
    table_t,
    sent0,
    sent1,
    sent2,
    got0,
    got1,
    got2,
    mix0,
    mix1,
    mix2,
    part0,
    part1,
    part2,
    own,
    measured,
    cuts,
    load_sem,
    film_send,
    film_recv,
    mix_send,
    mix_recv,
    own_send,
    own_recv,
    amp_send,
    amp_recv,
    meta_send,
    meta_recv,
    cut_send,
    pass_send,
    win_recv,
):
    strips, angle_devs, depths, layers, slots, columns = sizes
    quarter = strips // 4
    half = slots // depths
    share = WX // angle_devs
    reach = share + SHEAR
    sent = (sent0, sent1, sent2)
    got = (got0, got1, got2)
    mix = (mix0, mix1, mix2)
    parts = (part0, part1, part2)
    s = lax.axis_index("strip")
    a = lax.axis_index("angle")
    d = lax.axis_index("depth")
    meta = Meta(shear, owner_slot, slots, ())

    def rcopy(source, target, send_sem, recv_sem, **where):
        return pltpu.make_async_remote_copy(
            source, target, send_sem, recv_sem, device_id=where, device_id_type=MESH
        )

    def wrap(strip):
        return lax.rem(strip + 4 * strips, strips)

    loads = [
        pltpu.make_async_copy(
            crystal.at[layer, part],
            film.at[layer * WX : (layer + 1) * WX, part * columns : (part + 1) * columns],
            load_sem.at[layer * 2 + part],
        )
        for layer in range(layers)
        for part in range(2)
    ]
    late = [
        pltpu.make_async_copy(source, target, load_sem.at[2 * layers + i])
        for i, (source, target) in enumerate(
            ((probe_in, probe), (table_in, table), (table_t_in, table_t))
        )
    ]
    for copy in loads + late:
        copy.start()

    barrier = pltpu.get_barrier_semaphore()
    shifts = set()
    for k in range(REACHES):
        for t in range(quarter):
            shifts |= {(1 - k + 4 * t) % strips, (k - 1 - 4 * t) % strips}
    expected = jnp.int32(0)
    for shift in sorted(shifts | {0}):
        peer = wrap(s + shift)
        if quarter == 1 and shift:
            close = jnp.abs(peer - s) == 1
        else:
            close = peer >= 0
        near = angle_devs + depths - 1 - (1 if shift == 0 else 0)
        expected = expected + jnp.where(close, near, 0)

        @pl.when(close)
        def _():
            for step in range(angle_devs):
                if shift or step:
                    place = {"strip": peer, "angle": lax.rem(a + step, angle_devs)}
                    pl.semaphore_signal(barrier, 1, device_id=place, device_id_type=MESH)
            for step in range(1, depths):
                place = {"strip": peer, "depth": lax.rem(d + step, depths)}
                pl.semaphore_signal(barrier, 1, device_id=place, device_id_type=MESH)

    for copy in loads:
        copy.wait()

    def block(k, device):
        rows = ROWS[k] // depths
        return pl.ds(pl.multiple_of(device * rows, rows), rows)

    def mix_copy(k, q, step):
        target = lax.rem(d + step, depths)
        return rcopy(
            sent[k].at[q, block(k, target)],
            mix[k].at[q, step],
            mix_send.at[k, q, step],
            mix_recv.at[k, q, step],
            depth=target,
        )

    def film_copy(k, q):
        return rcopy(
            parts[k].at[q],
            got[k].at[q % half, block(k, d)],
            film_send.at[k, q],
            film_recv.at[k, d, q % half],
            strip=wrap(s - k + 4 * (q % quarter) + 1),
            depth=q // half,
        )

    def own_copy(q):
        return rcopy(
            sent[1].at[q],
            own.at[d, q % half],
            own_send.at[q],
            own_recv.at[d, q % half],
            depth=q // half,
        )

    def exchange(k, q):
        for step in range(1, depths):
            mix_copy(k, q, step).start()

    def merge(k, q):
        value = sent[k][q, block(k, d)].astype(jnp.float32)
        for step in range(1, depths):
            mix_copy(k, q, step).wait_recv()
            value = value + mix[k][q, step].astype(jnp.float32)
        parts[k][q] = value.astype(jnp.bfloat16)
        film_copy(k, q).start()

    def own_strip(k, q):
        return (1 - k + 4 * (q % quarter)) % strips == 0

    def project(k, q):
        home = s - k
        offset = meta.pick(scan_x, home, q) - WX * k + BASES[k]
        angle = meta.pick(slot_angle, home, q)
        corner = meta.pick(scan_y, home, q)
        gap = differences(ROWS[k], WX)
        picks = jnp.concatenate(
            [one_hot(gap == offset + meta.shear(angle, z)) for z in range(layers)], axis=1
        )
        tall = dot(picks, film[...]).astype(jnp.bfloat16)
        window = one_hot(differences(columns, FRAME) == -corner)
        return jnp.concatenate(
            [dot(tall[:, :columns], window), dot(tall[:, columns:], window)], axis=1
        ).astype(jnp.bfloat16)

    def reached(k):
        return (s - k >= 0) & (s - k <= strips - 3)

    for q in range(slots):
        for k in (0, 2):

            @pl.when(reached(k))
            def _():
                sent[k][q] = project(k, q)

        if q == 0:
            pl.semaphore_wait(barrier, expected)
        for k in (0, 2):

            @pl.when(reached(k))
            def _():
                exchange(k, q)

    for q in range(slots):
        for k in (0, 2):

            @pl.when(reached(k))
            def _():
                merge(k, q)

    def amp_copy(other):
        return rcopy(
            amplitude.at[other * half : (other + 1) * half],
            measured.at[d],
            amp_send.at[other],
            amp_recv.at[d],
            depth=other,
        )

    def amp_own(other):
        return pltpu.make_async_copy(
            amplitude.at[other * half : (other + 1) * half], measured.at[d], amp_recv.at[d]
        )

    tables = (
        (shear_in, shear_out),
        (scan_y_in, scan_y_out),
        (slot_angle_in, slot_angle_out),
        (owner_slot_in, owner_slot_out),
    )

    def meta_copies(step):
        return [
            rcopy(
                source,
                target.at[step],
                meta_send.at[step, i],
                meta_recv.at[step, i],
                angle=lax.rem(a + step, angle_devs),
            )
            for i, (source, target) in enumerate(tables)
        ]

    for other in range(depths):

        @pl.when(d != other)
        def _():
            amp_copy(other).start()

        @pl.when(d == other)
        def _():
            amp_own(other).start()

    for step in range(1, angle_devs):
        for copy in meta_copies(step):
            copy.start()

    @pl.when(reached(1))
    def _():
        for q in range(slots):
            sent[1][q] = project(1, q)
            if own_strip(1, q):

                @pl.when(d == q // half)
                def _():
                    own[d, q % half] = sent[1][q]

                @pl.when(d != q // half)
                def _():
                    own_copy(q).start()
            else:
                exchange(1, q)
        for q in range(slots):
            if not own_strip(1, q):
                merge(1, q)

    for copy in late:
        copy.wait()
    for other in range(depths):

        @pl.when(d != other)
        def _():
            rcopy(
                amplitude.at[other * half : (other + 1) * half],
                measured.at[other],
                amp_send.at[other],
                amp_recv.at[other],
                depth=other,
            ).wait_recv()

        @pl.when(d == other)
        def _():
            amp_own(other).wait()

    for lane in range(half):
        quota = d * half + lane
        home = wrap(s - 1 - 4 * lax.rem(quota, quarter))

        @pl.when(home <= strips - 3)
        def _():
            def arrive(k):
                for source in range(depths):
                    rows = ROWS[k] // depths
                    rcopy(
                        parts[k].at[lane],
                        got[k].at[lane, source * rows : (source + 1) * rows],
                        film_send.at[k, lane],
                        film_recv.at[k, source, lane],
                        strip=wrap(home + k),
                        depth=source,
                    ).wait_recv()

            local = wrap(home + 1) == s

            @pl.when(local)
            def _():
                value = own[d, lane].astype(jnp.float32)
                for step in range(1, depths):
                    source = lax.rem(d + step, depths)
                    rcopy(
                        sent[1].at[lane],
                        own.at[source, lane],
                        own_send.at[lane],
                        own_recv.at[source, lane],
                        depth=source,
                    ).wait_recv()
                    value = value + own[source, lane].astype(jnp.float32)
                got[1][lane] = value.astype(jnp.bfloat16)

            @pl.when(jnp.logical_not(local))
            def _():
                arrive(1)

            arrive(0)
            arrive(2)

            def gathered(ref, low, high):
                return ref[lane, low:high].astype(jnp.float32)

            whole = jnp.concatenate(
                [
                    gathered(got1, 0, WX) + gathered(got0, 0, WX),
                    gathered(got1, WX, FRAME) + gathered(got2, 0, FRAME - WX),
                ],
                axis=0,
            )
            probe_re = probe[0].astype(jnp.float32)
            probe_im = probe[1].astype(jnp.float32)
            film_re, film_im = whole[:, :FRAME], whole[:, FRAME:]
            exit_wave = jnp.concatenate(
                [probe_re * film_re - probe_im * film_im, probe_re * film_im + probe_im * film_re],
                axis=1,
            ).astype(jnp.bfloat16)
            section = dot(exit_wave, table[...]).astype(jnp.bfloat16)
            spectrum = dot(
                table_t[...], jnp.concatenate([section[:, :FRAME], section[:, FRAME:]], axis=0)
            )
            spec_re, spec_im = spectrum[:FRAME], spectrum[FRAME:]
            magnitude = jnp.sqrt(spec_re * spec_re + spec_im * spec_im)
            levels = jnp.concatenate(
                [measured[source, lane] for source in range(depths)], axis=0
            ).astype(jnp.float32)
            live = meta.slot(home, quota) < counts[0, home]
            live = jnp.where(live, 1.0, 0.0).astype(jnp.float32)
            factor = (1.0 - levels / jnp.maximum(magnitude, 1.0)) * live
            residual = jnp.concatenate([spec_re * factor, spec_im * factor], axis=1).astype(
                jnp.bfloat16
            )
            inverse = dot(residual, table_t[...]).astype(jnp.bfloat16)
            wave = dot(
                table[...], jnp.concatenate([inverse[:, :FRAME], inverse[:, FRAME:]], axis=0)
            )
            wave_re, wave_im = wave[:FRAME], wave[FRAME:]
            back = jnp.concatenate(
                [probe_re * wave_re + probe_im * wave_im, probe_re * wave_im - probe_im * wave_re],
                axis=1,
            ).astype(jnp.bfloat16)
            offset = meta.pick(scan_x, home, quota)
            gap = differences(reach, FRAME)
            for k in (2, 0, 1):
                for part in range(angle_devs):
                    first = WX * k - offset + part * share - (SHEAR - 1)
                    cuts[lane, k, part] = dot(one_hot(gap == first), back).astype(jnp.bfloat16)

    def cut_copy(k, q, home, step):
        target = lax.rem(a + step, angle_devs)
        return rcopy(
            cuts.at[q % half, k, target],
            windows.at[step, k, q],
            cut_send.at[k, q % half, step],
            win_recv.at[step, k, q],
            strip=wrap(home + k),
            angle=target,
        )

    def cut_local(k, q):
        return pltpu.make_async_copy(
            cuts.at[q % half, k, a], windows.at[0, k, q], win_recv.at[0, k, q]
        )

    def pass_copy(step, k, q, other):
        return rcopy(
            windows.at[step, k, q],
            windows.at[step, k, q],
            pass_send.at[step, k, q % half, other],
            win_recv.at[step, k, q],
            depth=other,
        )

    def sends(act):
        for q in range(slots):
            home = wrap(s - 1 - 4 * (q % quarter))

            @pl.when((home <= strips - 3) & (d == q // half))
            def _():
                for step in list(range(1, angle_devs)) + [0]:
                    for k in (0, 2, 1):
                        if not (step == 0 and own_strip(k, q)):
                            act(cut_copy(k, q, home, step))

    sends(lambda copy: copy.start())

    for q in range(slots):
        home = wrap(s - 1 - 4 * (q % quarter))
        for k in range(REACHES):
            if own_strip(k, q):

                @pl.when((home <= strips - 3) & (d == q // half))
                def _():
                    cut_local(k, q).start()

    def relays(act):
        for step in range(angle_devs):
            for k in range(REACHES):

                @pl.when(reached(k))
                def _():
                    for q in range(slots):

                        @pl.when(d == q // half)
                        def _():
                            act(step, k, q)

    def relay(step, k, q):
        if step == 0 and own_strip(k, q):
            cut_local(k, q).wait()
        else:
            cut_copy(k, q, s - k, step).wait_recv()
        for other in range(depths):
            if other != q // half:
                pass_copy(step, k, q, other).start()

    relays(relay)

    for step in range(angle_devs):
        for k in range(REACHES):

            @pl.when(reached(k))
            def _():
                for q in range(slots):

                    @pl.when(d != q // half)
                    def _():
                        pass_copy(step, k, q, q // half).wait_recv()

    for step in range(1, angle_devs):
        for copy in meta_copies(step):
            copy.wait_recv()

    for other in range(depths):

        @pl.when(d != other)
        def _():
            amp_copy(other).wait_send()

    for step in range(1, angle_devs):
        for copy in meta_copies(step):
            copy.wait_send()
    for k in range(REACHES):

        @pl.when(reached(k))
        def _():
            for q in range(slots):
                if own_strip(k, q):

                    @pl.when(d != q // half)
                    def _():
                        own_copy(q).wait_send()
                else:
                    film_copy(k, q).wait_send()
                    for step in range(1, depths):
                        mix_copy(k, q, step).wait_send()

    sends(lambda copy: copy.wait_send())

    def passed(step, k, q):
        for other in range(depths):
            if other != q // half:
                pass_copy(step, k, q, other).wait_send()

    relays(passed)


def deposit_kernel(
    sizes,
    scaling,
    windows,
    shear,
    scan_y,
    slot_angle,
    owner_slot,
    shears,
    scans_y,
    slot_angles,
    owner_slots,
    out,
    placed,
    total,
):
    strips, angle_devs, depths, layers, slots, columns = sizes
    share = WX // angle_devs
    reach = share + SHEAR
    stride = -(-reach // 128) * 128
    s = lax.axis_index("strip")
    first = jnp.maximum(s - strips + 3, 0)
    groups = [(Meta(shear, owner_slot, slots, ()), scan_y, slot_angle)]
    for step in range(1, angle_devs):
        groups.append((Meta(shears, owner_slots, slots, (step,)), scans_y, slot_angles))

    for i in range(angle_devs * slots):
        placed[i * stride + reach : (i + 1) * stride] = jnp.zeros(
            (stride - reach, 2 * columns), jnp.bfloat16
        )
    for k in range(REACHES):
        home = s - k

        @pl.when((home >= 0) & (home <= strips - 3))
        def _():
            lifts = []
            for step in range(angle_devs):
                meta, corners, angles = groups[step]
                for q in range(slots):
                    at = (step * slots + q) * stride
                    corner = meta.pick(corners, home, q)
                    value = windows[step, k, q].astype(jnp.float32)
                    margin = jnp.zeros((reach, columns - FRAME), jnp.float32)
                    for part in range(2):
                        wide = jnp.concatenate(
                            [value[:, part * FRAME : (part + 1) * FRAME], margin], axis=1
                        )
                        placed[at : at + reach, part * columns : (part + 1) * columns] = pltpu.roll(
                            wide, corner, 1
                        ).astype(jnp.bfloat16)
                    angle = meta.pick(angles, home, q)
                    lifts.append([meta.shear(angle, z) for z in range(layers)])
            gap = differences(share, stride)
            picks = jnp.concatenate(
                [
                    jnp.concatenate([one_hot(gap == SHEAR - 1 - lift[z]) for lift in lifts], axis=1)
                    for z in range(layers)
                ],
                axis=0,
            )

            @pl.when(first == k)
            def _():
                total[...] = dot(picks, placed[...])

            @pl.when(first != k)
            def _():
                total[...] += dot(picks, placed[...])

    for z in range(layers):
        for part in range(2):
            out[z, part] = (
                total[z * share : (z + 1) * share, part * columns : (part + 1) * columns] * scaling
            )


def body(sizes_of, crystal, probe, amplitude, shear, scan_x, scan_y, slot_angle, owner_slot, counts):
    strips, angle_devs, depths = sizes_of
    layers, _, _, columns = crystal.shape
    slots = owner_slot.shape[2]
    half = slots // depths
    share = WX // angle_devs
    reach = share + SHEAR
    stride = -(-reach // 128) * 128
    table, table_t = dft_tables()
    bf16 = jnp.bfloat16
    scan_x, scan_y, slot_angle, owner_slot = [
        jnp.swapaxes(value, 1, 2) for value in (scan_x, scan_y, slot_angle, owner_slot)
    ]
    sizes = (strips, angle_devs, depths, layers, slots, columns)
    tables = (shear, scan_y, slot_angle, owner_slot)
    anywhere = pl.BlockSpec(memory_space=pl.ANY)
    vmem = pl.BlockSpec(memory_space=pltpu.VMEM)
    smem = pl.BlockSpec(memory_space=pltpu.SMEM)
    dma = pltpu.SemaphoreType.DMA
    scratch = [
        pltpu.VMEM((layers * WX, 2 * columns), bf16),
        pltpu.VMEM(probe.shape, bf16),
        pltpu.VMEM(table.shape, bf16),
        pltpu.VMEM(table.shape, bf16),
    ]
    scratch += [pltpu.VMEM((slots, rows, 2 * FRAME), bf16) for rows in ROWS]
    scratch += [pltpu.VMEM((half, rows, 2 * FRAME), bf16) for rows in ROWS]
    scratch += [pltpu.VMEM((slots, depths, rows // depths, 2 * FRAME), bf16) for rows in ROWS]
    scratch += [pltpu.VMEM((slots, rows // depths, 2 * FRAME), bf16) for rows in ROWS]
    scratch += [pltpu.VMEM((depths, half, FRAME, 2 * FRAME), bf16)]
    scratch += [
        pltpu.VMEM((depths, half, FRAME // depths, FRAME), bf16),
        pltpu.VMEM((half, REACHES, angle_devs, reach, 2 * FRAME), bf16),
        dma((2 * layers + 3,)),
        dma((REACHES, slots)),
        dma((REACHES, depths, half)),
        dma((REACHES, slots, depths)),
        dma((REACHES, slots, depths)),
        dma((slots,)),
        dma((depths, half)),
        dma((depths,)),
        dma((depths,)),
        dma((angle_devs, len(tables))),
        dma((angle_devs, len(tables))),
        dma((REACHES, half, angle_devs)),
        dma((angle_devs, REACHES, half, depths)),
        dma((angle_devs, REACHES, slots)),
    ]
    windows, *others = pl.pallas_call(
        functools.partial(kernel, sizes),
        out_shape=(
            jax.ShapeDtypeStruct((angle_devs, REACHES, slots, reach, 2 * FRAME), bf16),
        )
        + tuple(jax.ShapeDtypeStruct((angle_devs,) + x.shape, jnp.int32) for x in tables),
        in_specs=[anywhere] * 5 + [smem] * 6 + [anywhere] * 4,
        out_specs=(anywhere,) * 5,
        scratch_shapes=scratch,
        compiler_params=pltpu.CompilerParams(collective_id=0, has_side_effects=True),
    )(
        crystal,
        probe,
        amplitude,
        table,
        table_t,
        shear,
        scan_x,
        scan_y,
        slot_angle,
        owner_slot,
        counts,
        *tables,
    )
    scaling = 1.0 / (shear.shape[0] * angle_devs)
    return pl.pallas_call(
        functools.partial(deposit_kernel, sizes, scaling),
        out_shape=jax.ShapeDtypeStruct((layers, 2, share, columns), jnp.float32),
        in_specs=[vmem] + [smem] * 8,
        out_specs=vmem,
        scratch_shapes=[
            pltpu.VMEM((angle_devs * slots * stride, 2 * columns), bf16),
            pltpu.VMEM((layers * share, 2 * columns), jnp.float32),
        ],
    )(windows, *tables, *others)


def solution(mesh):
    placed = (
        P(("groups", "depth"), None, "strip", None),
        P(),
        P("angle", ("groups", "strip", "depth"), None),
        P(("groups", "angle"), "depth"),
        P(("groups", "angle"), None, None),
        P(("groups", "angle"), None, None),
        P(("groups", "angle"), None, None),
        P(("groups", "angle"), None, None),
        P(("groups", "angle"), None),
    )
    sizes_of = (mesh.shape["strip"], mesh.shape["angle"], mesh.shape["depth"])
    return jax.shard_map(
        functools.partial(body, sizes_of),
        mesh=mesh,
        in_specs=placed,
        out_specs=P(("groups", "depth"), None, ("strip", "angle"), None),
        check_vma=False,
    )
```

profile of v0, /device:TPU:0, one launch (start us, length us, event | category | flops | bytes accessed | tf_op | source)
XLA Modules:
  0.0 23.3 jit_solution(9596852965407301351)
XLA Ops:
  0.0 20.5 %shard_map.109 = (bf16[2,3,2,80,512]{4,3,2,1,0:T(8,128)(2,1)}, s32[2,4,4]{2,1,0:T(4,128)}, s32[2,1,2,4]{3,2,1,0:T(2,128)}, s32[2,1,2,4]{3,2,1,0:T(2,128)}, s32[2,1,2,4]{3,2,1,0:T(2,128)}) custom-call(bf16[4,2,128,384]{3,2,1,0:T(8,128)(2,1)} %crystal.1, bf16[2,256,256]{2,1,0:T(8,128)(2,1)} %probe_in.1, bf16[2,128,256]{2,1,0:T(8,128)(2,1)} %amplitude.1, ...), custom_call_target="tpu_custom_call" | custom-call | tf_op jit(solution)/shard_map/pallas_call | solution.py:694
  20.5 2.8 %shard_map.110 = f32[4,2,64,384]{3,2,1,0:T(8,128)} custom-call(bf16[2,3,2,80,512]{4,3,2,1,0:T(8,128)(2,1)} %get-tuple-element.10.windows, s32[4,4]{1,0:T(4,128)} %shear.3, s32[1,2,4]{2,1,0:T(2,128)} %bitcast.6, s32[1,2,4]{2,1,0:T(2,128)} %bitcast.9, s32[1,2,4]{2,1,0:T(2,128)} %bitcast.12, s32[2,4,4]{2,1,0:T(4,128)} %get-tuple-element.11.shears, ...), custom_call_target="tpu_custom_call" | custom-call | tf_op jit(solution)/shard_map/pallas_call | solution.py:719
where the time goes:
time: 23.5 us; the launch traced here: 23.3 us
  Pallas kernels  23.3 us (99%)
    pallas_call x1, Pallas kernels, body(): pl.pallas_call(functools.partial(kernel, sizes), out_shape=(jax.ShapeDtyp...  20.5 us
    pallas_call x1, Pallas kernels, body(): pl.pallas_call(functools.partial(deposit_kernel, sizes, scaling), out_sha...  2.79 us

commit v1 on v0

v1 whole, which is shorter than its diff:
```python
import functools

import jax
import jax.numpy as jnp
import numpy as np
from jax import lax
from jax.experimental import pallas as pl
from jax.experimental.pallas import tpu as pltpu
from jax.sharding import PartitionSpec as P

FRAME = 256
WX = 128
SHEAR = 16
REACHES = 3
ROWS = (WX, FRAME, FRAME - WX)
BASES = (0, 0, WX)
VMEM_LIMIT = 44 * 2**20
MESH = pl.DeviceIdType.MESH


def dft_tables():
    index_row = np.arange(FRAME)
    phase = (index_row[:, None] * index_row[None, :] % FRAME) * (2.0 * np.pi / FRAME)
    real = np.cos(phase) / np.sqrt(FRAME)
    imag = -np.sin(phase) / np.sqrt(FRAME)
    table = np.block([[real, imag], [-imag, real]]).astype(np.float32)
    return jnp.asarray(table, jnp.bfloat16), jnp.asarray(table.T, jnp.bfloat16)


def dot(left, right):
    return jnp.dot(left, right, preferred_element_type=jnp.float32)


def differences(rows, columns):
    shape = (rows, columns)
    return lax.broadcasted_iota(jnp.int32, shape, 1) - lax.broadcasted_iota(jnp.int32, shape, 0)


def one_hot(mask):
    return jnp.where(mask, 1.0, 0.0).astype(jnp.bfloat16)


class Meta:
    def __init__(self, lifts, owner_slot, slots, lead):
        self.lifts, self.owner_slot = lifts, owner_slot
        self.slots, self.lead = slots, lead

    def shear(self, angle, z):
        return self.lifts[self.lead + (angle, z)]

    def pick(self, ref, home, quota):
        value = jnp.int32(0)
        for m in range(self.slots):
            at = self.lead + (0, m, home)
            value = value + jnp.where(self.owner_slot[at] == quota, ref[at], 0)
        return value

    def slot(self, home, quota):
        value = jnp.int32(0)
        for m in range(self.slots):
            at = self.lead + (0, m, home)
            value = value + jnp.where(self.owner_slot[at] == quota, m, 0)
        return value


def kernel(
    sizes,
    scaling,
    crystal,
    probe_in,
    amplitude,
    table_in,
    table_t_in,
    shear_in,
    scan_x_in,
    scan_y_in,
    slot_angle_in,
    owner_slot_in,
    counts_in,
    out,
    shear_out,
    scan_y_out,
    slot_angle_out,
    owner_slot_out,
    shear,
    scan_x,
    scan_y,
    slot_angle,
    owner_slot,
    counts,
    shears,
    scans_y,
    slot_angles,
    owner_slots,
    film,
    probe,
    table,
    table_t,
    sent0,
    sent1,
    sent2,
    got0,
    got1,
    got2,
    mix0,
    mix1,
    mix2,
    part0,
    part1,
    part2,
    own,
    measured,
    cuts,
    windows,
    spreads,
    picks,
    placed,
    spec,
    back,
    load_sem,
    film_send,
    film_recv,
    mix_send,
    mix_recv,
    own_send,
    own_recv,
    amp_send,
    amp_recv,
    meta_load,
    meta_send,
    meta_recv,
    meta_pull,
    cut_send,
    pass_send,
    win_recv,
):
    strips, angle_devs, depths, layers, slots, columns = sizes
    quarter = strips // 4
    half = slots // depths
    share = WX // angle_devs
    reach = share + SHEAR
    sent = (sent0, sent1, sent2)
    got = (got0, got1, got2)
    mix = (mix0, mix1, mix2)
    parts = (part0, part1, part2)
    s = lax.axis_index("strip")
    a = lax.axis_index("angle")
    d = lax.axis_index("depth")
    meta = Meta(shear, owner_slot, slots, ())

    def rcopy(source, target, send_sem, recv_sem, **where):
        return pltpu.make_async_remote_copy(
            source, target, send_sem, recv_sem, device_id=where, device_id_type=MESH
        )

    def wrap(strip):
        return lax.rem(strip + 4 * strips, strips)

    metas = [
        pltpu.make_async_copy(source, target, meta_load.at[i])
        for i, (source, target) in enumerate(
            (
                (shear_in, shear),
                (scan_x_in, scan_x),
                (scan_y_in, scan_y),
                (slot_angle_in, slot_angle),
                (owner_slot_in, owner_slot),
                (counts_in, counts),
            )
        )
    ]
    loads = [
        pltpu.make_async_copy(
            crystal.at[layer, part],
            film.at[layer * WX : (layer + 1) * WX, part * columns : (part + 1) * columns],
            load_sem.at[layer * 2 + part],
        )
        for layer in range(layers)
        for part in range(2)
    ]
    late = [
        pltpu.make_async_copy(source, target, load_sem.at[2 * layers + i])
        for i, (source, target) in enumerate(
            ((probe_in, probe), (table_in, table), (table_t_in, table_t))
        )
    ]
    for copy in metas + loads:
        copy.start()

    barrier = pltpu.get_barrier_semaphore()
    shifts = set()
    for k in range(REACHES):
        for t in range(quarter):
            shifts |= {(1 - k + 4 * t) % strips, (k - 1 - 4 * t) % strips}
    expected = jnp.int32(0)
    for shift in sorted(shifts | {0}):
        peer = wrap(s + shift)
        if quarter == 1 and shift:
            close = jnp.abs(peer - s) == 1
        else:
            close = peer >= 0
        near = angle_devs + depths - 1 - (1 if shift == 0 else 0)
        expected = expected + jnp.where(close, near, 0)

        @pl.when(close)
        def _():
            for step in range(angle_devs):
                if shift or step:
                    place = {"strip": peer, "angle": lax.rem(a + step, angle_devs)}
                    pl.semaphore_signal(barrier, 1, device_id=place, device_id_type=MESH)
            for step in range(1, depths):
                place = {"strip": peer, "depth": lax.rem(d + step, depths)}
                pl.semaphore_signal(barrier, 1, device_id=place, device_id_type=MESH)

    out[...] = jnp.zeros(out.shape, jnp.float32)
    placed[...] = jnp.zeros(placed.shape, jnp.bfloat16)

    for copy in metas + loads:
        copy.wait()
    for copy in late:
        copy.start()

    def block(k, device):
        rows = ROWS[k] // depths
        return pl.ds(pl.multiple_of(device * rows, rows), rows)

    def mix_copy(k, q, step):
        target = lax.rem(d + step, depths)
        return rcopy(
            sent[k].at[q, block(k, target)],
            mix[k].at[q, step],
            mix_send.at[k, q, step],
            mix_recv.at[k, q, step],
            depth=target,
        )

    def film_copy(k, q):
        return rcopy(
            parts[k].at[q],
            got[k].at[q % half, block(k, d)],
            film_send.at[k, q],
            film_recv.at[k, d, q % half],
            strip=wrap(s - k + 4 * (q % quarter) + 1),
            depth=q // half,
        )

    def own_copy(q):
        return rcopy(
            sent[1].at[q],
            own.at[d, q % half],
            own_send.at[q],
            own_recv.at[d, q % half],
            depth=q // half,
        )

    def exchange(k, q):
        for step in range(1, depths):
            mix_copy(k, q, step).start()

    def merge(k, q):
        value = sent[k][q, block(k, d)].astype(jnp.float32)
        for step in range(1, depths):
            mix_copy(k, q, step).wait_recv()
            value = value + mix[k][q, step].astype(jnp.float32)
        parts[k][q] = value.astype(jnp.bfloat16)
        film_copy(k, q).start()

    def own_strip(k, q):
        return (1 - k + 4 * (q % quarter)) % strips == 0

    def project(k, q):
        home = s - k
        offset = meta.pick(scan_x, home, q) - WX * k + BASES[k]
        angle = meta.pick(slot_angle, home, q)
        corner = meta.pick(scan_y, home, q)
        gap = differences(ROWS[k], WX)
        chosen = jnp.concatenate(
            [one_hot(gap == offset + meta.shear(angle, z)) for z in range(layers)], axis=1
        )
        tall = dot(chosen, film[...]).astype(jnp.bfloat16)
        window = one_hot(differences(columns, FRAME) == -corner)
        return jnp.concatenate(
            [dot(tall[:, :columns], window), dot(tall[:, columns:], window)], axis=1
        ).astype(jnp.bfloat16)

    def reached(k):
        return (s - k >= 0) & (s - k <= strips - 3)

    for q in range(slots):
        for k in (0, 2):

            @pl.when(reached(k))
            def _():
                sent[k][q] = project(k, q)
                if q or k:
                    exchange(k, q)

            if q == 0 and k == 0:
                pl.semaphore_wait(barrier, expected)

                @pl.when(reached(0))
                def _():
                    exchange(0, 0)


    def amp_copy(other):
        return rcopy(
            amplitude.at[other * half : (other + 1) * half],
            measured.at[d],
            amp_send.at[other],
            amp_recv.at[d],
            depth=other,
        )

    def amp_own(other):
        return pltpu.make_async_copy(
            amplitude.at[other * half : (other + 1) * half], measured.at[d], amp_recv.at[d]
        )

    tables = (
        (shear_in, shear_out, shears),
        (scan_y_in, scan_y_out, scans_y),
        (slot_angle_in, slot_angle_out, slot_angles),
        (owner_slot_in, owner_slot_out, owner_slots),
    )

    def meta_copies(step):
        return [
            rcopy(
                source,
                target.at[step],
                meta_send.at[step, i],
                meta_recv.at[step, i],
                angle=lax.rem(a + step, angle_devs),
            )
            for i, (source, target, _) in enumerate(tables)
        ]

    def meta_pulls(step):
        return [
            pltpu.make_async_copy(target.at[step], local.at[step], meta_pull.at[step, i])
            for i, (_, target, local) in enumerate(tables)
        ]

    for step in range(1, angle_devs):
        for copy in meta_copies(step):
            copy.start()

    for other in range(depths):

        @pl.when(d != other)
        def _():
            amp_copy(other).start()

        @pl.when(d == other)
        def _():
            amp_own(other).start()

    for q in range(slots):
        for k in (0, 2):

            @pl.when(reached(k))
            def _():
                merge(k, q)


    @pl.when(reached(1))
    def _():
        for q in range(slots):
            sent[1][q] = project(1, q)
            if own_strip(1, q):

                @pl.when(d == q // half)
                def _():
                    own[d, q % half] = sent[1][q]

                @pl.when(d != q // half)
                def _():
                    own_copy(q).start()
            else:
                exchange(1, q)
        for q in range(slots):
            if not own_strip(1, q):
                merge(1, q)

    groups = [(meta, scan_y, slot_angle)]
    for step in range(1, angle_devs):
        lead = (step,)
        groups.append((Meta(shears, owner_slots, slots, lead), scans_y, slot_angles))
    depth_rows = placed.shape[0]

    def prepare(step, k):
        home = s - k
        source, corners, angles = groups[step]
        lifts = []
        for q in range(slots):
            corner = source.pick(corners, home, q)
            spreads[step, k, q] = one_hot(differences(FRAME, columns) == corner)
            angle = source.pick(angles, home, q)
            lifts.append([source.shear(angle, z) for z in range(layers)])
        gap = differences(share, depth_rows)
        for z in range(layers):
            mask = gap == SHEAR - 1 - lifts[0][z]
            for q in range(1, slots):
                mask = mask | (gap == q * reach + SHEAR - 1 - lifts[q][z])
            picks[step, k, z * share : (z + 1) * share] = one_hot(mask)

    for k in range(REACHES):

        @pl.when(reached(k))
        def _():
            prepare(0, k)

    for copy in late:
        copy.wait()
    for other in range(depths):

        @pl.when(d != other)
        def _():
            rcopy(
                amplitude.at[other * half : (other + 1) * half],
                measured.at[other],
                amp_send.at[other],
                amp_recv.at[other],
                depth=other,
            ).wait_recv()

        @pl.when(d == other)
        def _():
            amp_own(other).wait()


    def cut_copy(k, lane, quota, home, step):
        target = lax.rem(a + step, angle_devs)
        return rcopy(
            cuts.at[lane, k, target],
            windows.at[step, k, quota],
            cut_send.at[k, lane, step],
            win_recv.at[step, k, quota],
            strip=wrap(home + k),
            angle=target,
        )

    def owned(act):
        for lane in range(half):
            quota = d * half + lane
            home = wrap(s - 1 - 4 * lax.rem(quota, quarter))

            @pl.when(home <= strips - 3)
            def _():
                act(lane, quota, home, wrap(home + 1) == s)

    def dispatch(k, lane, quota, home, local, act):
        for step in list(range(1, angle_devs)) + [0]:
            if k == 1 and step == 0:

                @pl.when(jnp.logical_not(local))
                def _():
                    act(cut_copy(k, lane, quota, home, step))
            else:
                act(cut_copy(k, lane, quota, home, step))

    def work(lane, quota, home, local):
        def arrive(k):
            for source in range(depths):
                rows = ROWS[k] // depths
                rcopy(
                    parts[k].at[lane],
                    got[k].at[lane, source * rows : (source + 1) * rows],
                    film_send.at[k, lane],
                    film_recv.at[k, source, lane],
                    strip=wrap(home + k),
                    depth=source,
                ).wait_recv()

        @pl.when(local)
        def _():
            value = own[d, lane].astype(jnp.float32)
            for step in range(1, depths):
                source = lax.rem(d + step, depths)
                rcopy(
                    sent[1].at[lane],
                    own.at[source, lane],
                    own_send.at[lane],
                    own_recv.at[source, lane],
                    depth=source,
                ).wait_recv()
                value = value + own[source, lane].astype(jnp.float32)
            got[1][lane] = value.astype(jnp.bfloat16)

        @pl.when(jnp.logical_not(local))
        def _():
            arrive(1)

        def forward(low, high, extra):
            rows = slice(low, high)
            whole = got1[lane, rows].astype(jnp.float32) + extra.astype(jnp.float32)
            re, im = whole[:, :FRAME], whole[:, FRAME:]
            probe_re = probe[0, rows].astype(jnp.float32)
            probe_im = probe[1, rows].astype(jnp.float32)
            exit_wave = jnp.concatenate(
                [probe_re * re - probe_im * im, probe_re * im + probe_im * re], axis=1
            ).astype(jnp.bfloat16)
            section = dot(exit_wave, table[...]).astype(jnp.bfloat16)
            left = jnp.concatenate(
                [table_t[:, rows], table_t[:, FRAME + low : FRAME + high]], axis=1
            )
            return dot(left, jnp.concatenate([section[:, :FRAME], section[:, FRAME:]], axis=0))

        arrive(0)
        spec[...] = forward(0, WX, got0[lane])
        arrive(2)
        spectrum = spec[...] + forward(WX, FRAME, got2[lane])
        spec_re, spec_im = spectrum[:FRAME], spectrum[FRAME:]
        magnitude = jnp.sqrt(spec_re * spec_re + spec_im * spec_im)
        levels = jnp.concatenate(
            [measured[source, lane] for source in range(depths)], axis=0
        ).astype(jnp.float32)
        live = meta.slot(home, quota) < counts[0, home]
        live = jnp.where(live, 1.0, 0.0).astype(jnp.float32)
        factor = (1.0 - levels / jnp.maximum(magnitude, 1.0)) * live
        residual = jnp.concatenate([spec_re * factor, spec_im * factor], axis=1).astype(
            jnp.bfloat16
        )
        inverse = dot(residual, table_t[...]).astype(jnp.bfloat16)
        stacked = jnp.concatenate([inverse[:, :FRAME], inverse[:, FRAME:]], axis=0)
        offset = meta.pick(scan_x, home, quota)

        def backward(low, high):
            rows = slice(low, high)
            left = jnp.concatenate([table[rows], table[FRAME + low : FRAME + high]], axis=0)
            wave = dot(left, stacked)
            re, im = wave[: high - low], wave[high - low :]
            probe_re = probe[0, rows].astype(jnp.float32)
            probe_im = probe[1, rows].astype(jnp.float32)
            return jnp.concatenate(
                [probe_re * re + probe_im * im, probe_re * im - probe_im * re], axis=1
            ).astype(jnp.bfloat16)

        def cut(k, low, value):
            gap = differences(reach, value.shape[0])
            for part in range(angle_devs):
                first = WX * k - offset + part * share - (SHEAR - 1) - low
                cuts[lane, k, part] = dot(one_hot(gap == first), value).astype(jnp.bfloat16)

        top = backward(0, WX)
        back[0:WX] = top
        cut(0, 0, top)
        dispatch(0, lane, quota, home, local, lambda copy: copy.start())
        bottom = backward(WX, FRAME)
        back[WX:FRAME] = bottom
        cut(2, WX, bottom)
        dispatch(2, lane, quota, home, local, lambda copy: copy.start())
        cut(1, 0, back[...])
        dispatch(1, lane, quota, home, local, lambda copy: copy.start())

        @pl.when(local)
        def _():
            windows[0, 1, quota] = cuts[lane, 1, a]


    owned(work)

    for step in range(1, angle_devs):
        for copy in meta_copies(step):
            copy.wait_recv()
        for copy in meta_pulls(step):
            copy.start()
    for step in range(1, angle_devs):
        for copy in meta_pulls(step):
            copy.wait()
    for step in range(1, angle_devs):
        for k in range(REACHES):

            @pl.when(reached(k))
            def _():
                prepare(step, k)


    def pass_copy(step, k, q, other):
        return rcopy(
            windows.at[step, k, q],
            windows.at[step, k, q],
            pass_send.at[step, k, q % half, other],
            win_recv.at[step, k, q],
            depth=other,
        )

    def relay(step, k):
        for q in range(slots):

            @pl.when(d == q // half)
            def _():
                if not (step == 0 and own_strip(k, q)):
                    cut_copy(k, q % half, q, s - k, step).wait_recv()
                for other in range(depths):
                    if other != q // half:
                        pass_copy(step, k, q, other).start()

    def place(step, k, q, at):
        value = windows[step, k, q]
        spread = spreads[step, k, q]
        for part in range(2):
            placed[pl.ds(pl.multiple_of(at, 16), reach), part * columns : (part + 1) * columns] = dot(
                value[:, part * FRAME : (part + 1) * FRAME], spread
            ).astype(jnp.bfloat16)

    def deposit(step, k):
        for lane in range(half):
            q = d * half + lane
            place(step, k, q, q * reach)
        for q in range(slots):

            @pl.when(d != q // half)
            def _():
                pass_copy(step, k, q, q // half).wait_recv()
                place(step, k, q, q * reach)

        value = dot(picks[step, k], placed[...]) * scaling
        for z in range(layers):
            for part in range(2):
                out[z, part] += value[
                    z * share : (z + 1) * share, part * columns : (part + 1) * columns
                ]

    order = [(0, 1)] + [(step, 1) for step in range(1, angle_devs)]
    order += [(step, k) for step in list(range(1, angle_devs)) + [0] for k in (0, 2)]
    for i in range(len(order) + 1):
        if i < len(order):
            step, k = order[i]

            @pl.when(reached(k))
            def _():
                relay(step, k)

        if i:
            step, k = order[i - 1]

            @pl.when(reached(k))
            def _():
                deposit(step, k)

    for other in range(depths):

        @pl.when(d != other)
        def _():
            amp_copy(other).wait_send()

    for step in range(1, angle_devs):
        for copy in meta_copies(step):
            copy.wait_send()
    for k in range(REACHES):

        @pl.when(reached(k))
        def _():
            for q in range(slots):
                if own_strip(k, q):

                    @pl.when(d != q // half)
                    def _():
                        own_copy(q).wait_send()
                else:
                    film_copy(k, q).wait_send()
                    for step in range(1, depths):
                        mix_copy(k, q, step).wait_send()

    def drain(lane, quota, home, local):
        for k in range(REACHES):
            dispatch(k, lane, quota, home, local, lambda copy: copy.wait_send())

    owned(drain)

    for step, k in order:

        @pl.when(reached(k))
        def _():
            for q in range(slots):

                @pl.when(d == q // half)
                def _():
                    for other in range(depths):
                        if other != q // half:
                            pass_copy(step, k, q, other).wait_send()


def body(sizes_of, crystal, probe, amplitude, shear, scan_x, scan_y, slot_angle, owner_slot, counts):
    strips, angle_devs, depths = sizes_of
    layers, _, _, columns = crystal.shape
    slots = owner_slot.shape[2]
    half = slots // depths
    share = WX // angle_devs
    reach = share + SHEAR
    depth_rows = -(-(slots * reach) // 128) * 128
    table, table_t = dft_tables()
    bf16 = jnp.bfloat16
    scan_x, scan_y, slot_angle, owner_slot = [
        jnp.swapaxes(value, 1, 2) for value in (scan_x, scan_y, slot_angle, owner_slot)
    ]
    sizes = (strips, angle_devs, depths, layers, slots, columns)
    tables = (shear, scan_y, slot_angle, owner_slot)
    hbm = pl.BlockSpec(memory_space=pltpu.HBM)
    vmem = pl.BlockSpec(memory_space=pltpu.VMEM)
    dma = pltpu.SemaphoreType.DMA
    small = (shear, scan_x, scan_y, slot_angle, owner_slot, counts)
    scratch = [pltpu.SMEM(x.shape, jnp.int32) for x in small]
    scratch += [pltpu.SMEM((angle_devs,) + x.shape, jnp.int32) for x in tables]
    scratch += [
        pltpu.VMEM((layers * WX, 2 * columns), bf16),
        pltpu.VMEM(probe.shape, bf16),
        pltpu.VMEM(table.shape, bf16),
        pltpu.VMEM(table.shape, bf16),
    ]
    scratch += [pltpu.VMEM((slots, rows, 2 * FRAME), bf16) for rows in ROWS]
    scratch += [pltpu.VMEM((half, rows, 2 * FRAME), bf16) for rows in ROWS]
    scratch += [pltpu.VMEM((slots, depths, rows // depths, 2 * FRAME), bf16) for rows in ROWS]
    scratch += [pltpu.VMEM((slots, rows // depths, 2 * FRAME), bf16) for rows in ROWS]
    scratch += [pltpu.VMEM((depths, half, FRAME, 2 * FRAME), bf16)]
    scratch += [
        pltpu.VMEM((depths, half, FRAME // depths, FRAME), bf16),
        pltpu.VMEM((half, REACHES, angle_devs, reach, 2 * FRAME), bf16),
        pltpu.VMEM((angle_devs, REACHES, slots, reach, 2 * FRAME), bf16),
        pltpu.VMEM((angle_devs, REACHES, slots, FRAME, columns), bf16),
        pltpu.VMEM((angle_devs, REACHES, layers * share, depth_rows), bf16),
        pltpu.VMEM((depth_rows, 2 * columns), bf16),
        pltpu.VMEM((2 * FRAME, FRAME), jnp.float32),
        pltpu.VMEM((FRAME, 2 * FRAME), bf16),
        dma((2 * layers + 3,)),
        dma((REACHES, slots)),
        dma((REACHES, depths, half)),
        dma((REACHES, slots, depths)),
        dma((REACHES, slots, depths)),
        dma((slots,)),
        dma((depths, half)),
        dma((depths,)),
        dma((depths,)),
        dma((len(small),)),
        dma((angle_devs, len(tables))),
        dma((angle_devs, len(tables))),
        dma((angle_devs, len(tables))),
        dma((REACHES, half, angle_devs)),
        dma((angle_devs, REACHES, half, depths)),
        dma((angle_devs, REACHES, slots)),
    ]
    scaling = 1.0 / (shear.shape[0] * angle_devs)
    result, *_ = pl.pallas_call(
        functools.partial(kernel, sizes, scaling),
        out_shape=(jax.ShapeDtypeStruct((layers, 2, share, columns), jnp.float32),)
        + tuple(jax.ShapeDtypeStruct((angle_devs,) + x.shape, jnp.int32) for x in tables),
        in_specs=[hbm] * 11,
        out_specs=(vmem,) + (hbm,) * 4,
        scratch_shapes=scratch,
        compiler_params=pltpu.CompilerParams(
            collective_id=0, has_side_effects=True, vmem_limit_bytes=VMEM_LIMIT
        ),
    )(
        *(
            pltpu.with_memory_space_constraint(x, pltpu.HBM)
            for x in (crystal, probe, amplitude, table, table_t, *small)
        )
    )
    return result


def solution(mesh):
    placed = (
        P(("groups", "depth"), None, "strip", None),
        P(),
        P("angle", ("groups", "strip", "depth"), None),
        P(("groups", "angle"), "depth"),
        P(("groups", "angle"), None, None),
        P(("groups", "angle"), None, None),
        P(("groups", "angle"), None, None),
        P(("groups", "angle"), None, None),
        P(("groups", "angle"), None),
    )
    sizes_of = (mesh.shape["strip"], mesh.shape["angle"], mesh.shape["depth"])
    return jax.shard_map(
        functools.partial(body, sizes_of),
        mesh=mesh,
        in_specs=placed,
        out_specs=P(("groups", "depth"), None, ("strip", "angle"), None),
        check_vma=False,
    )
```

time: 23.5 us -> 21.7 us (0.923)
  the two profiles are of different devices: /device:TPU:0 before, /device:TPU:9 now
where the time goes in v1:
time: 21.7 us; the launch traced here: 21.5 us
  Pallas kernels  20.6 us (95%)
  local copies, waits for them, and re-layouts  0.88 us (4%)
    pallas_call x1, Pallas kernels, body(): pl.pallas_call(functools.partial(kernel, sizes, scaling), out_shape=(jax....  20.6 us
    unnamed x1, local copies, waits for them, and re-layouts  0.88 us

profile of v1, /device:TPU:9, one launch (start us, length us, event | category | flops | bytes accessed | tf_op | source)
XLA Modules:
  0.0 21.5 jit_solution(10619134820634288070)
XLA Ops:
  0.0 20.6 %shard_map.109 = (f32[4,2,64,384]{3,2,1,0:T(8,128)S(1)}, s32[2,4,4]{2,1,0:T(4,128)}, s32[2,1,2,4]{3,2,1,0:T(2,128)}, s32[2,1,2,4]{3,2,1,0:T(2,128)}, s32[2,1,2,4]{3,2,1,0:T(2,128)}) custom-call(bf16[4,2,128,384]{3,2,1,0:T(8,128)(2,1)} %crystal.1, bf16[2,256,256]{2,1,0:T(8,128)(2,1)} %probe_in.1, bf16[2,128,256]{2,1,0:T(8,128)(2,1)} %amplitude.1, ...), custom_call_target="tpu_custom_call" | custom-call | tf_op jit(solution)/shard_map/pallas_call | solution.py:745
  20.6 0.9 %copy.13 = f32[4,2,64,384]{3,2,1,0:T(8,128)} copy(f32[4,2,64,384]{3,2,1,0:T(8,128)S(1)} %get-tuple-element.6) | data formatting | bytes 1572864

commit v2 on v1

--- a/solution.py
+++ b/solution.py
@@ -24,7 +24,7 @@
     real = np.cos(phase) / np.sqrt(FRAME)
     imag = -np.sin(phase) / np.sqrt(FRAME)
     table = np.block([[real, imag], [-imag, real]]).astype(np.float32)
-    return jnp.asarray(table, jnp.bfloat16), jnp.asarray(table.T, jnp.bfloat16)
+    return jnp.asarray(np.stack([table, table.T]), jnp.bfloat16)
 
 
 def dot(left, right):
@@ -69,8 +69,7 @@
     crystal,
     probe_in,
     amplitude,
-    table_in,
-    table_t_in,
+    tables_in,
     shear_in,
     scan_x_in,
     scan_y_in,
@@ -94,8 +93,7 @@
     owner_slots,
     film,
     probe,
-    table,
-    table_t,
+    dft,
     sent0,
     sent1,
     sent2,
@@ -112,7 +110,8 @@
     measured,
     cuts,
     windows,
-    spreads,
+    dft_rot,
+    probe_rot,
     picks,
     placed,
     spec,
@@ -147,6 +146,10 @@
     a = lax.axis_index("angle")
     d = lax.axis_index("depth")
     meta = Meta(shear, owner_slot, slots, ())
+    margin = columns - FRAME
+
+    def lanes(rows):
+        return lax.broadcasted_iota(jnp.int32, (rows, margin), 1)
 
     def rcopy(source, target, send_sem, recv_sem, **where):
         return pltpu.make_async_remote_copy(
@@ -171,19 +174,17 @@
     ]
     loads = [
         pltpu.make_async_copy(
-            crystal.at[layer, part],
-            film.at[layer * WX : (layer + 1) * WX, part * columns : (part + 1) * columns],
-            load_sem.at[layer * 2 + part],
-        )
-        for layer in range(layers)
+            crystal.at[:, part],
+            film.at[:, :, part * columns : (part + 1) * columns],
+            load_sem.at[0],
+        )
         for part in range(2)
     ]
     late = [
-        pltpu.make_async_copy(source, target, load_sem.at[2 * layers + i])
-        for i, (source, target) in enumerate(
-            ((probe_in, probe), (table_in, table), (table_t_in, table_t))
-        )
+        pltpu.make_async_copy(source, target, load_sem.at[1 + i])
+        for i, (source, target) in enumerate(((probe_in, probe), (tables_in, dft)))
     ]
+    table, table_t = dft.at[0], dft.at[1]
     for copy in metas + loads:
         copy.start()
 
@@ -215,8 +216,9 @@
     out[...] = jnp.zeros(out.shape, jnp.float32)
     placed[...] = jnp.zeros(placed.shape, jnp.bfloat16)
 
-    for copy in metas + loads:
+    for copy in metas:
         copy.wait()
+    pltpu.make_async_copy(film, film, load_sem.at[0]).wait()
     for copy in late:
         copy.start()
 
@@ -228,9 +230,9 @@
         target = lax.rem(d + step, depths)
         return rcopy(
             sent[k].at[q, block(k, target)],
-            mix[k].at[q, step],
-            mix_send.at[k, q, step],
-            mix_recv.at[k, q, step],
+            mix[k].at[q, step - 1],
+            mix_send.at[k, step - 1],
+            mix_recv.at[k, q, step - 1],
             depth=target,
         )
 
@@ -238,8 +240,8 @@
         return rcopy(
             parts[k].at[q],
             got[k].at[q % half, block(k, d)],
-            film_send.at[k, q],
-            film_recv.at[k, d, q % half],
+            film_send.at[k],
+            film_recv.at[k, q % half],
             strip=wrap(s - k + 4 * (q % quarter) + 1),
             depth=q // half,
         )
@@ -261,46 +263,53 @@
         value = sent[k][q, block(k, d)].astype(jnp.float32)
         for step in range(1, depths):
             mix_copy(k, q, step).wait_recv()
-            value = value + mix[k][q, step].astype(jnp.float32)
+            value = value + mix[k][q, step - 1].astype(jnp.float32)
         parts[k][q] = value.astype(jnp.bfloat16)
         film_copy(k, q).start()
 
     def own_strip(k, q):
         return (1 - k + 4 * (q % quarter)) % strips == 0
 
-    def project(k, q):
+    def project(k):
         home = s - k
-        offset = meta.pick(scan_x, home, q) - WX * k + BASES[k]
-        angle = meta.pick(slot_angle, home, q)
-        corner = meta.pick(scan_y, home, q)
         gap = differences(ROWS[k], WX)
-        chosen = jnp.concatenate(
-            [one_hot(gap == offset + meta.shear(angle, z)) for z in range(layers)], axis=1
-        )
-        tall = dot(chosen, film[...]).astype(jnp.bfloat16)
-        window = one_hot(differences(columns, FRAME) == -corner)
-        return jnp.concatenate(
-            [dot(tall[:, :columns], window), dot(tall[:, columns:], window)], axis=1
-        ).astype(jnp.bfloat16)
+        chosen = []
+        for q in range(slots):
+            offset = meta.pick(scan_x, home, q) - WX * k + BASES[k]
+            angle = meta.pick(slot_angle, home, q)
+            chosen.append(
+                jnp.concatenate(
+                    [one_hot(gap == offset + meta.shear(angle, z)) for z in range(layers)], axis=1
+                )
+            )
+        flat = film[...].reshape(layers * WX, 2 * columns)
+        tall = dot(jnp.concatenate(chosen, axis=0), flat)
+        for q in range(slots):
+            corner = meta.pick(scan_y, home, q)
+            first = lanes(ROWS[k]) >= corner
+            rows = tall[q * ROWS[k] : (q + 1) * ROWS[k]]
+            wound = []
+            for part in range(2):
+                side = rows[:, part * columns : (part + 1) * columns]
+                wound += [jnp.where(first, side[:, :margin], side[:, FRAME:]), side[:, margin:FRAME]]
+            sent[k][q] = jnp.concatenate(wound, axis=1).astype(jnp.bfloat16)
 
     def reached(k):
         return (s - k >= 0) & (s - k <= strips - 3)
 
-    for q in range(slots):
-        for k in (0, 2):
-
-            @pl.when(reached(k))
-            def _():
-                sent[k][q] = project(k, q)
-                if q or k:
-                    exchange(k, q)
-
-            if q == 0 and k == 0:
-                pl.semaphore_wait(barrier, expected)
-
-                @pl.when(reached(0))
-                def _():
-                    exchange(0, 0)
+    for k in (0, 2):
+
+        @pl.when(reached(k))
+        def _():
+            project(k)
+
+    pl.semaphore_wait(barrier, expected)
+    for k in (0, 2):
+
+        @pl.when(reached(k))
+        def _():
+            for q in range(slots):
+                exchange(k, q)
 
 
     def amp_copy(other):
@@ -308,13 +317,13 @@
             amplitude.at[other * half : (other + 1) * half],
             measured.at[d],
             amp_send.at[other],
-            amp_recv.at[d],
+            amp_recv.at[0],
             depth=other,
         )
 
     def amp_own(other):
         return pltpu.make_async_copy(
-            amplitude.at[other * half : (other + 1) * half], measured.at[d], amp_recv.at[d]
+            amplitude.at[other * half : (other + 1) * half], measured.at[d], amp_recv.at[0]
         )
 
     tables = (
@@ -329,8 +338,8 @@
             rcopy(
                 source,
                 target.at[step],
-                meta_send.at[step, i],
-                meta_recv.at[step, i],
+                meta_send.at[step - 1, i],
+                meta_recv.at[step - 1, i],
                 angle=lax.rem(a + step, angle_devs),
             )
             for i, (source, target, _) in enumerate(tables)
@@ -338,7 +347,7 @@
 
     def meta_pulls(step):
         return [
-            pltpu.make_async_copy(target.at[step], local.at[step], meta_pull.at[step, i])
+            pltpu.make_async_copy(target.at[step], local.at[step], meta_pull.at[step - 1, i])
             for i, (_, target, local) in enumerate(tables)
         ]
 
@@ -366,8 +375,8 @@
 
     @pl.when(reached(1))
     def _():
+        project(1)
         for q in range(slots):
-            sent[1][q] = project(1, q)
             if own_strip(1, q):
 
                 @pl.when(d == q // half)
@@ -391,11 +400,9 @@
 
     def prepare(step, k):
         home = s - k
-        source, corners, angles = groups[step]
+        source, _, angles = groups[step]
         lifts = []
         for q in range(slots):
-            corner = source.pick(corners, home, q)
-            spreads[step, k, q] = one_hot(differences(FRAME, columns) == corner)
             angle = source.pick(angles, home, q)
             lifts.append([source.shear(angle, z) for z in range(layers)])
         gap = differences(share, depth_rows)
@@ -413,21 +420,7 @@
 
     for copy in late:
         copy.wait()
-    for other in range(depths):
-
-        @pl.when(d != other)
-        def _():
-            rcopy(
-                amplitude.at[other * half : (other + 1) * half],
-                measured.at[other],
-                amp_send.at[other],
-                amp_recv.at[other],
-                depth=other,
-            ).wait_recv()
-
-        @pl.when(d == other)
-        def _():
-            amp_own(other).wait()
+    pltpu.make_async_copy(measured, measured, amp_recv.at[0]).wait()
 
 
     def cut_copy(k, lane, quota, home, step):
@@ -435,7 +428,7 @@
         return rcopy(
             cuts.at[lane, k, target],
             windows.at[step, k, quota],
-            cut_send.at[k, lane, step],
+            cut_send.at[k, lane],
             win_recv.at[step, k, quota],
             strip=wrap(home + k),
             angle=target,
@@ -462,16 +455,17 @@
 
     def work(lane, quota, home, local):
         def arrive(k):
-            for source in range(depths):
-                rows = ROWS[k] // depths
-                rcopy(
-                    parts[k].at[lane],
-                    got[k].at[lane, source * rows : (source + 1) * rows],
-                    film_send.at[k, lane],
-                    film_recv.at[k, source, lane],
-                    strip=wrap(home + k),
-                    depth=source,
-                ).wait_recv()
+            pltpu.make_async_copy(got[k].at[lane], got[k].at[lane], film_recv.at[k, lane]).wait()
+
+        corner = meta.pick(scan_y, home, quota)
+        gap = differences(FRAME, FRAME)
+        turn = one_hot((gap == -corner) | (gap == FRAME - corner))
+        back_turn = one_hot((gap == corner) | (gap == corner - FRAME))
+        for part in range(2):
+            at = slice(part * FRAME, (part + 1) * FRAME)
+            probe_rot[lane, part] = dot(probe[part], back_turn).astype(jnp.bfloat16)
+            dft_rot[lane, 0, at] = dot(turn, table[at]).astype(jnp.bfloat16)
+            dft_rot[lane, 1, :, at] = dot(table_t[:, at], back_turn).astype(jnp.bfloat16)
 
         @pl.when(local)
         def _():
@@ -496,12 +490,12 @@
             rows = slice(low, high)
             whole = got1[lane, rows].astype(jnp.float32) + extra.astype(jnp.float32)
             re, im = whole[:, :FRAME], whole[:, FRAME:]
-            probe_re = probe[0, rows].astype(jnp.float32)
-            probe_im = probe[1, rows].astype(jnp.float32)
+            probe_re = probe_rot[lane, 0, rows].astype(jnp.float32)
+            probe_im = probe_rot[lane, 1, rows].astype(jnp.float32)
             exit_wave = jnp.concatenate(
                 [probe_re * re - probe_im * im, probe_re * im + probe_im * re], axis=1
             ).astype(jnp.bfloat16)
-            section = dot(exit_wave, table[...]).astype(jnp.bfloat16)
+            section = dot(exit_wave, dft_rot[lane, 0]).astype(jnp.bfloat16)
             left = jnp.concatenate(
                 [table_t[:, rows], table_t[:, FRAME + low : FRAME + high]], axis=1
             )
@@ -522,7 +516,7 @@
         residual = jnp.concatenate([spec_re * factor, spec_im * factor], axis=1).astype(
             jnp.bfloat16
         )
-        inverse = dot(residual, table_t[...]).astype(jnp.bfloat16)
+        inverse = dot(residual, dft_rot[lane, 1]).astype(jnp.bfloat16)
         stacked = jnp.concatenate([inverse[:, :FRAME], inverse[:, FRAME:]], axis=0)
         offset = meta.pick(scan_x, home, quota)
 
@@ -531,28 +525,30 @@
             left = jnp.concatenate([table[rows], table[FRAME + low : FRAME + high]], axis=0)
             wave = dot(left, stacked)
             re, im = wave[: high - low], wave[high - low :]
-            probe_re = probe[0, rows].astype(jnp.float32)
-            probe_im = probe[1, rows].astype(jnp.float32)
+            probe_re = probe_rot[lane, 0, rows].astype(jnp.float32)
+            probe_im = probe_rot[lane, 1, rows].astype(jnp.float32)
             return jnp.concatenate(
                 [probe_re * re + probe_im * im, probe_re * im - probe_im * re], axis=1
             ).astype(jnp.bfloat16)
 
-        def cut(k, low, value):
+        def cut(k, part, low, value):
             gap = differences(reach, value.shape[0])
-            for part in range(angle_devs):
-                first = WX * k - offset + part * share - (SHEAR - 1) - low
-                cuts[lane, k, part] = dot(one_hot(gap == first), value).astype(jnp.bfloat16)
+            first = WX * k - offset + part * share - (SHEAR - 1) - low
+            cuts[lane, k, part] = dot(one_hot(gap == first), value).astype(jnp.bfloat16)
 
         top = backward(0, WX)
         back[0:WX] = top
-        cut(0, 0, top)
+        for part in range(angle_devs):
+            cut(0, part, 0, top)
         dispatch(0, lane, quota, home, local, lambda copy: copy.start())
         bottom = backward(WX, FRAME)
         back[WX:FRAME] = bottom
-        cut(2, WX, bottom)
+        for part in range(angle_devs):
+            cut(1, part, 0, back[...])
+        dispatch(1, lane, quota, home, local, lambda copy: copy.start())
+        for part in range(angle_devs):
+            cut(2, part, WX, bottom)
         dispatch(2, lane, quota, home, local, lambda copy: copy.start())
-        cut(1, 0, back[...])
-        dispatch(1, lane, quota, home, local, lambda copy: copy.start())
 
         @pl.when(local)
         def _():
@@ -581,7 +577,7 @@
         return rcopy(
             windows.at[step, k, q],
             windows.at[step, k, q],
-            pass_send.at[step, k, q % half, other],
+            pass_send.at[k, other],
             win_recv.at[step, k, q],
             depth=other,
         )
@@ -598,12 +594,19 @@
                         pass_copy(step, k, q, other).start()
 
     def place(step, k, q, at):
-        value = windows[step, k, q]
-        spread = spreads[step, k, q]
+        source, corners, _ = groups[step]
+        first = lanes(reach) >= source.pick(corners, s - k, q)
+        rows = pl.ds(pl.multiple_of(at, 16), reach)
         for part in range(2):
-            placed[pl.ds(pl.multiple_of(at, 16), reach), part * columns : (part + 1) * columns] = dot(
-                value[:, part * FRAME : (part + 1) * FRAME], spread
-            ).astype(jnp.bfloat16)
+            head = windows[step, k, q, :, part * FRAME : part * FRAME + margin].astype(jnp.float32)
+            left = part * columns
+            placed[rows, left : left + margin] = jnp.where(first, head, 0.0).astype(jnp.bfloat16)
+            placed[rows, left + margin : left + FRAME] = windows[
+                step, k, q, :, part * FRAME + margin : (part + 1) * FRAME
+            ]
+            placed[rows, left + FRAME : left + columns] = jnp.where(first, 0.0, head).astype(
+                jnp.bfloat16
+            )
 
     def deposit(step, k):
         for lane in range(half):
@@ -623,22 +626,25 @@
                     z * share : (z + 1) * share, part * columns : (part + 1) * columns
                 ]
 
-    order = [(0, 1)] + [(step, 1) for step in range(1, angle_devs)]
-    order += [(step, k) for step in list(range(1, angle_devs)) + [0] for k in (0, 2)]
-    for i in range(len(order) + 1):
-        if i < len(order):
-            step, k = order[i]
+    later = range(1, angle_devs)
+    stages = [[(0, 1)], [(step, 1) for step in later]]
+    stages += [[(step, k) for step in later for k in (0, 2)], [(0, 0), (0, 2)]]
+
+    def run(act, stage):
+        for step, k in stages[stage]:
 
             @pl.when(reached(k))
             def _():
-                relay(step, k)
-
-        if i:
-            step, k = order[i - 1]
-
-            @pl.when(reached(k))
-            def _():
-                deposit(step, k)
+                act(step, k)
+
+    run(relay, 0)
+    run(deposit, 0)
+    run(relay, 1)
+    run(relay, 2)
+    run(deposit, 1)
+    run(relay, 3)
+    run(deposit, 2)
+    run(deposit, 3)
 
     for other in range(depths):
 
@@ -659,28 +665,41 @@
                     @pl.when(d != q // half)
                     def _():
                         own_copy(q).wait_send()
-                else:
-                    film_copy(k, q).wait_send()
-                    for step in range(1, depths):
-                        mix_copy(k, q, step).wait_send()
+            rest = [q for q in range(slots) if not own_strip(k, q)]
+            if rest:
+                whole = parts[k].at[slots - len(rest) :]
+                pltpu.make_async_copy(whole, whole, film_send.at[k]).wait()
+                for step in range(1, depths):
+                    pltpu.make_async_copy(whole, whole, mix_send.at[k, step - 1]).wait()
 
     def drain(lane, quota, home, local):
         for k in range(REACHES):
-            dispatch(k, lane, quota, home, local, lambda copy: copy.wait_send())
+            whole = cuts.at[lane, k]
+            if k == 1:
+                most = cuts.at[lane, k, 1:]
+
+                @pl.when(local)
+                def _():
+                    pltpu.make_async_copy(most, most, cut_send.at[k, lane]).wait()
+
+                @pl.when(jnp.logical_not(local))
+                def _():
+                    pltpu.make_async_copy(whole, whole, cut_send.at[k, lane]).wait()
+            else:
+                pltpu.make_async_copy(whole, whole, cut_send.at[k, lane]).wait()
 
     owned(drain)
 
-    for step, k in order:
+    for k in range(REACHES):
 
         @pl.when(reached(k))
         def _():
-            for q in range(slots):
-
-                @pl.when(d == q // half)
+            for other in range(depths):
+
+                @pl.when(d != other)
                 def _():
-                    for other in range(depths):
-                        if other != q // half:
-                            pass_copy(step, k, q, other).wait_send()
+                    whole = windows.at[:, k, 0:half]
+                    pltpu.make_async_copy(whole, whole, pass_send.at[k, other]).wait()
 
 
 def body(sizes_of, crystal, probe, amplitude, shear, scan_x, scan_y, slot_angle, owner_slot, counts):
@@ -691,7 +710,7 @@
     share = WX // angle_devs
     reach = share + SHEAR
     depth_rows = -(-(slots * reach) // 128) * 128
-    table, table_t = dft_tables()
+    dft = dft_tables()
     bf16 = jnp.bfloat16
     scan_x, scan_y, slot_angle, owner_slot = [
         jnp.swapaxes(value, 1, 2) for value in (scan_x, scan_y, slot_angle, owner_slot)
@@ -705,40 +724,40 @@
     scratch = [pltpu.SMEM(x.shape, jnp.int32) for x in small]
     scratch += [pltpu.SMEM((angle_devs,) + x.shape, jnp.int32) for x in tables]
     scratch += [
-        pltpu.VMEM((layers * WX, 2 * columns), bf16),
+        pltpu.VMEM((layers, WX, 2 * columns), bf16),
         pltpu.VMEM(probe.shape, bf16),
-        pltpu.VMEM(table.shape, bf16),
-        pltpu.VMEM(table.shape, bf16),
+        pltpu.VMEM(dft.shape, bf16),
     ]
     scratch += [pltpu.VMEM((slots, rows, 2 * FRAME), bf16) for rows in ROWS]
     scratch += [pltpu.VMEM((half, rows, 2 * FRAME), bf16) for rows in ROWS]
-    scratch += [pltpu.VMEM((slots, depths, rows // depths, 2 * FRAME), bf16) for rows in ROWS]
+    scratch += [pltpu.VMEM((slots, depths - 1, rows // depths, 2 * FRAME), bf16) for rows in ROWS]
     scratch += [pltpu.VMEM((slots, rows // depths, 2 * FRAME), bf16) for rows in ROWS]
     scratch += [pltpu.VMEM((depths, half, FRAME, 2 * FRAME), bf16)]
     scratch += [
         pltpu.VMEM((depths, half, FRAME // depths, FRAME), bf16),
         pltpu.VMEM((half, REACHES, angle_devs, reach, 2 * FRAME), bf16),
         pltpu.VMEM((angle_devs, REACHES, slots, reach, 2 * FRAME), bf16),
-        pltpu.VMEM((angle_devs, REACHES, slots, FRAME, columns), bf16),
+        pltpu.VMEM((half,) + dft.shape, bf16),
+        pltpu.VMEM((half,) + probe.shape, bf16),
         pltpu.VMEM((angle_devs, REACHES, layers * share, depth_rows), bf16),
         pltpu.VMEM((depth_rows, 2 * columns), bf16),
         pltpu.VMEM((2 * FRAME, FRAME), jnp.float32),
         pltpu.VMEM((FRAME, 2 * FRAME), bf16),
-        dma((2 * layers + 3,)),
-        dma((REACHES, slots)),
-        dma((REACHES, depths, half)),
-        dma((REACHES, slots, depths)),
-        dma((REACHES, slots, depths)),
+        dma((3,)),
+        dma((REACHES,)),
+        dma((REACHES, half)),
+        dma((REACHES, depths - 1)),
+        dma((REACHES, slots, depths - 1)),
         dma((slots,)),
         dma((depths, half)),
         dma((depths,)),
-        dma((depths,)),
+        dma((1,)),
         dma((len(small),)),
-        dma((angle_devs, len(tables))),
-        dma((angle_devs, len(tables))),
-        dma((angle_devs, len(tables))),
-        dma((REACHES, half, angle_devs)),
-        dma((angle_devs, REACHES, half, depths)),
+        dma((angle_devs - 1, len(tables))),
+        dma((angle_devs - 1, len(tables))),
+        dma((angle_devs - 1, len(tables))),
+        dma((REACHES, half)),
+        dma((REACHES, depths)),
         dma((angle_devs, REACHES, slots)),
     ]
     scaling = 1.0 / (shear.shape[0] * angle_devs)
@@ -746,7 +765,7 @@
         functools.partial(kernel, sizes, scaling),
         out_shape=(jax.ShapeDtypeStruct((layers, 2, share, columns), jnp.float32),)
         + tuple(jax.ShapeDtypeStruct((angle_devs,) + x.shape, jnp.int32) for x in tables),
-        in_specs=[hbm] * 11,
+        in_specs=[hbm] * 10,
         out_specs=(vmem,) + (hbm,) * 4,
         scratch_shapes=scratch,
         compiler_params=pltpu.CompilerParams(
@@ -755,7 +774,7 @@
     )(
         *(
             pltpu.with_memory_space_constraint(x, pltpu.HBM)
-            for x in (crystal, probe, amplitude, table, table_t, *small)
+            for x in (crystal, probe, amplitude, dft, *small)
         )
     )
     return result

time: 21.7 us -> 19.7 us (0.908)
  Pallas kernels: 20.6 us -> 18.6 us
    pallas_call x1, Pallas kernels: 20.6 us -> 18.6 us  [body(): pl.pallas_call(functools.partial(kernel, sizes, scaling), out_shape=(jax....]
where the time goes in v2:
time: 19.7 us; the launch traced here: 19.5 us
  Pallas kernels  18.6 us (94%)
  local copies, waits for them, and re-layouts  0.88 us (4%)
    pallas_call x1, Pallas kernels, body(): pl.pallas_call(functools.partial(kernel, sizes, scaling), out_shape=(jax....  18.6 us
    unnamed x1, local copies, waits for them, and re-layouts  0.88 us

profile of v2, /device:TPU:9, one launch (start us, length us, event | category | flops | bytes accessed | tf_op | source)
XLA Modules:
  0.0 19.5 jit_solution(14959715523235633191)
XLA Ops:
  0.0 18.6 %shard_map.100 = (f32[4,2,64,384]{3,2,1,0:T(8,128)S(1)}, s32[2,4,4]{2,1,0:T(4,128)}, s32[2,1,2,4]{3,2,1,0:T(2,128)}, s32[2,1,2,4]{3,2,1,0:T(2,128)}, s32[2,1,2,4]{3,2,1,0:T(2,128)}) custom-call(bf16[4,2,128,384]{3,2,1,0:T(8,128)(2,1)} %crystal.1, bf16[2,256,256]{2,1,0:T(8,128)(2,1)} %probe_in.1, bf16[2,128,256]{2,1,0:T(8,128)(2,1)} %amplitude.1, ...), custom_call_target="tpu_custom_call" | custom-call | tf_op jit(solution)/shard_map/pallas_call | solution.py:764
  18.6 0.9 %copy.12 = f32[4,2,64,384]{3,2,1,0:T(8,128)} copy(f32[4,2,64,384]{3,2,1,0:T(8,128)S(1)} %get-tuple-element.6) | data formatting | bytes 1572864

commit v3 on v2

--- a/solution.py
+++ b/solution.py
@@ -61,6 +61,15 @@
             at = self.lead + (0, m, home)
             value = value + jnp.where(self.owner_slot[at] == quota, m, 0)
         return value
+
+
+def bands(strips):
+    return REACHES if strips - 3 >= 2 else 2
+
+
+def batch_of(strips, angle_devs):
+    every = [(step, k) for step in range(angle_devs) for k in range(bands(strips))]
+    return [item for item in every if item != (0, 1)]
 
 
 def kernel(
@@ -112,8 +121,12 @@
     windows,
     dft_rot,
     probe_rot,
-    picks,
-    placed,
+    picks_local,
+    picks_mine,
+    picks_theirs,
+    placed_local,
+    placed_mine,
+    placed_theirs,
     spec,
     back,
     load_sem,
@@ -147,6 +160,16 @@
     d = lax.axis_index("depth")
     meta = Meta(shear, owner_slot, slots, ())
     margin = columns - FRAME
+    kinds = bands(strips)
+    batch = batch_of(strips, angle_devs)
+    rows_of = dict(zip(batch, range(len(batch))))
+
+    def kind(k):
+        return k % kinds
+
+    def seat(device):
+        return 0 if depths == 2 else device
+
 
     def lanes(rows):
         return lax.broadcasted_iota(jnp.int32, (rows, margin), 1)
@@ -214,7 +237,8 @@
                 pl.semaphore_signal(barrier, 1, device_id=place, device_id_type=MESH)
 
     out[...] = jnp.zeros(out.shape, jnp.float32)
-    placed[...] = jnp.zeros(placed.shape, jnp.bfloat16)
+    for ref in (placed_local, placed_mine, placed_theirs):
+        ref[...] = jnp.zeros(ref.shape, jnp.bfloat16)
 
     for copy in metas:
         copy.wait()
@@ -231,8 +255,8 @@
         return rcopy(
             sent[k].at[q, block(k, target)],
             mix[k].at[q, step - 1],
-            mix_send.at[k, step - 1],
-            mix_recv.at[k, q, step - 1],
+            mix_send.at[kind(k), step - 1],
+            mix_recv.at[kind(k), q, step - 1],
             depth=target,
         )
 
@@ -240,7 +264,7 @@
         return rcopy(
             parts[k].at[q],
             got[k].at[q % half, block(k, d)],
-            film_send.at[k],
+            film_send.at[kind(k)],
             film_recv.at[k, q % half],
             strip=wrap(s - k + 4 * (q % quarter) + 1),
             depth=q // half,
@@ -250,8 +274,8 @@
         return rcopy(
             sent[1].at[q],
             own.at[d, q % half],
-            own_send.at[q],
-            own_recv.at[d, q % half],
+            own_send.at[q % half, seat(q // half)],
+            own_recv.at[q % half, seat(d)],
             depth=q // half,
         )
 
@@ -316,7 +340,7 @@
         return rcopy(
             amplitude.at[other * half : (other + 1) * half],
             measured.at[d],
-            amp_send.at[other],
+            amp_send.at[seat(other)],
             amp_recv.at[0],
             depth=other,
         )
@@ -396,42 +420,49 @@
     for step in range(1, angle_devs):
         lead = (step,)
         groups.append((Meta(shears, owner_slots, slots, lead), scans_y, slot_angles))
-    depth_rows = placed.shape[0]
-
-    def prepare(step, k):
-        home = s - k
-        source, _, angles = groups[step]
-        lifts = []
-        for q in range(slots):
+
+    def prepare(target, items):
+        wanted = []
+        for step, k, q, at in items:
+            home = jnp.clip(s - k, 0, strips - 1)
+            source, _, angles = groups[step]
             angle = source.pick(angles, home, q)
-            lifts.append([source.shear(angle, z) for z in range(layers)])
-        gap = differences(share, depth_rows)
+            base = jnp.where(reached(k), at + SHEAR, -4 * target.shape[1])
+            wanted.append([base - source.shear(angle, z) for z in range(layers)])
+        gap = differences(share, target.shape[1])
         for z in range(layers):
-            mask = gap == SHEAR - 1 - lifts[0][z]
-            for q in range(1, slots):
-                mask = mask | (gap == q * reach + SHEAR - 1 - lifts[q][z])
-            picks[step, k, z * share : (z + 1) * share] = one_hot(mask)
-
-    for k in range(REACHES):
-
-        @pl.when(reached(k))
-        def _():
-            prepare(0, k)
+            mask = gap == wanted[0][z]
+            for want in wanted[1:]:
+                mask = mask | (gap == want[z])
+            target[z * share : (z + 1) * share] = one_hot(mask)
+
+    locals_ = [(0, 1, q, q * reach) for q in range(slots)]
+
+    def items_of(depth):
+        return [
+            (step, k, depth * half + lane, (lane * len(batch) + rows_of[step, kind(k)]) * reach)
+            for lane in range(half)
+            for step in list(range(1, angle_devs)) + [0]
+            for k in (1, 0, 2)
+            if (step, k) != (0, 1)
+        ]
+
+    prepare(picks_local, locals_)
 
     for copy in late:
         copy.wait()
     pltpu.make_async_copy(measured, measured, amp_recv.at[0]).wait()
 
 
-    def cut_copy(k, lane, quota, home, step):
-        target = lax.rem(a + step, angle_devs)
+    def cut_copy(k, lane, quota, home, part):
+        step = lax.rem(part - a + angle_devs, angle_devs)
         return rcopy(
-            cuts.at[lane, k, target],
-            windows.at[step, k, quota],
+            cuts.at[lane, k, part],
+            windows.at[step, kind(k), quota],
             cut_send.at[k, lane],
-            win_recv.at[step, k, quota],
+            win_recv.at[step, kind(k), quota],
             strip=wrap(home + k),
-            angle=target,
+            angle=part,
         )
 
     def owned(act):
@@ -442,16 +473,6 @@
             @pl.when(home <= strips - 3)
             def _():
                 act(lane, quota, home, wrap(home + 1) == s)
-
-    def dispatch(k, lane, quota, home, local, act):
-        for step in list(range(1, angle_devs)) + [0]:
-            if k == 1 and step == 0:
-
-                @pl.when(jnp.logical_not(local))
-                def _():
-                    act(cut_copy(k, lane, quota, home, step))
-            else:
-                act(cut_copy(k, lane, quota, home, step))
 
     def work(lane, quota, home, local):
         def arrive(k):
@@ -475,8 +496,8 @@
                 rcopy(
                     sent[1].at[lane],
                     own.at[source, lane],
-                    own_send.at[lane],
-                    own_recv.at[source, lane],
+                    own_send.at[lane, seat(source)],
+                    own_recv.at[lane, seat(source)],
                     depth=source,
                 ).wait_recv()
                 value = value + own[source, lane].astype(jnp.float32)
@@ -533,26 +554,32 @@
 
         def cut(k, part, low, value):
             gap = differences(reach, value.shape[0])
-            first = WX * k - offset + part * share - (SHEAR - 1) - low
+            first = WX * k - offset + part * share - SHEAR - low
             cuts[lane, k, part] = dot(one_hot(gap == first), value).astype(jnp.bfloat16)
+
+        def send(k, low, value):
+            for part in range(angle_devs):
+                cut(k, part, low, value)
+                copy = cut_copy(k, lane, quota, home, part)
+                if k == 1:
+
+                    @pl.when(jnp.logical_not(local & (a == part)))
+                    def _():
+                        copy.start()
+                else:
+                    copy.start()
 
         top = backward(0, WX)
         back[0:WX] = top
-        for part in range(angle_devs):
-            cut(0, part, 0, top)
-        dispatch(0, lane, quota, home, local, lambda copy: copy.start())
+        send(0, 0, top)
         bottom = backward(WX, FRAME)
         back[WX:FRAME] = bottom
-        for part in range(angle_devs):
-            cut(1, part, 0, back[...])
-        dispatch(1, lane, quota, home, local, lambda copy: copy.start())
-        for part in range(angle_devs):
-            cut(2, part, WX, bottom)
-        dispatch(2, lane, quota, home, local, lambda copy: copy.start())
+        send(1, 0, back[...])
+        send(2, WX, bottom)
 
         @pl.when(local)
         def _():
-            windows[0, 1, quota] = cuts[lane, 1, a]
+            windows[0, kind(1), quota] = cuts[lane, 1, a]
 
 
     owned(work)
@@ -565,22 +592,25 @@
     for step in range(1, angle_devs):
         for copy in meta_pulls(step):
             copy.wait()
-    for step in range(1, angle_devs):
-        for k in range(REACHES):
-
-            @pl.when(reached(k))
-            def _():
-                prepare(step, k)
+    mine = items_of(d)
+    theirs = [items_of(lax.rem(d + step, depths)) for step in range(1, depths)]
+    prepare(picks_mine, mine)
+    for step in range(1, depths):
+        prepare(picks_theirs.at[step - 1], theirs[step - 1])
 
 
     def pass_copy(step, k, q, other):
         return rcopy(
-            windows.at[step, k, q],
-            windows.at[step, k, q],
-            pass_send.at[k, other],
-            win_recv.at[step, k, q],
+            windows.at[step, kind(k), q],
+            windows.at[step, kind(k), q],
+            pass_send.at[kind(k), seat(other)],
+            win_recv.at[step, kind(k), q],
             depth=other,
         )
+
+    def recv(step, k, q):
+        window = windows.at[step, kind(k), q]
+        pltpu.make_async_copy(window, window, win_recv.at[step, kind(k), q]).wait()
 
     def relay(step, k):
         for q in range(slots):
@@ -588,63 +618,68 @@
             @pl.when(d == q // half)
             def _():
                 if not (step == 0 and own_strip(k, q)):
-                    cut_copy(k, q % half, q, s - k, step).wait_recv()
+                    recv(step, k, q)
                 for other in range(depths):
                     if other != q // half:
                         pass_copy(step, k, q, other).start()
 
-    def place(step, k, q, at):
+    def place(target, step, k, q, at):
         source, corners, _ = groups[step]
         first = lanes(reach) >= source.pick(corners, s - k, q)
-        rows = pl.ds(pl.multiple_of(at, 16), reach)
+        window = windows.at[step, kind(k), q]
+        rows = slice(at, at + reach)
         for part in range(2):
-            head = windows[step, k, q, :, part * FRAME : part * FRAME + margin].astype(jnp.float32)
+            head = window[:, part * FRAME : part * FRAME + margin].astype(jnp.float32)
             left = part * columns
-            placed[rows, left : left + margin] = jnp.where(first, head, 0.0).astype(jnp.bfloat16)
-            placed[rows, left + margin : left + FRAME] = windows[
-                step, k, q, :, part * FRAME + margin : (part + 1) * FRAME
+            target[rows, left : left + margin] = jnp.where(first, head, 0.0).astype(jnp.bfloat16)
+            target[rows, left + margin : left + FRAME] = window[
+                :, part * FRAME + margin : (part + 1) * FRAME
             ]
-            placed[rows, left + FRAME : left + columns] = jnp.where(first, 0.0, head).astype(
+            target[rows, left + FRAME : left + columns] = jnp.where(first, 0.0, head).astype(
                 jnp.bfloat16
             )
 
-    def deposit(step, k):
-        for lane in range(half):
-            q = d * half + lane
-            place(step, k, q, q * reach)
-        for q in range(slots):
-
-            @pl.when(d != q // half)
-            def _():
-                pass_copy(step, k, q, q // half).wait_recv()
-                place(step, k, q, q * reach)
-
-        value = dot(picks[step, k], placed[...]) * scaling
+    def add(chosen, target):
+        value = dot(chosen[...], target[...]) * scaling
         for z in range(layers):
             for part in range(2):
                 out[z, part] += value[
                     z * share : (z + 1) * share, part * columns : (part + 1) * columns
                 ]
 
-    later = range(1, angle_devs)
-    stages = [[(0, 1)], [(step, 1) for step in later]]
-    stages += [[(step, k) for step in later for k in (0, 2)], [(0, 0), (0, 2)]]
-
-    def run(act, stage):
-        for step, k in stages[stage]:
+    @pl.when(reached(1))
+    def _():
+        relay(0, 1)
+        for q in range(slots):
+
+            @pl.when(d != q // half)
+            def _():
+                pass_copy(0, 1, q, q // half).wait_recv()
+
+        for item in locals_:
+            place(placed_local, *item)
+        add(picks_local, placed_local)
+
+    for step, k in [(step, k) for step in list(range(1, angle_devs)) + [0] for k in (1, 0, 2)]:
+        if (step, k) != (0, 1):
 
             @pl.when(reached(k))
             def _():
-                act(step, k)
-
-    run(relay, 0)
-    run(deposit, 0)
-    run(relay, 1)
-    run(relay, 2)
-    run(deposit, 1)
-    run(relay, 3)
-    run(deposit, 2)
-    run(deposit, 3)
+                relay(step, k)
+                for item in mine:
+                    if item[:2] == (step, k):
+                        place(placed_mine, *item)
+
+    add(picks_mine, placed_mine)
+    for i in range(1, depths):
+        for step, k, q, at in theirs[i - 1]:
+
+            @pl.when(reached(k))
+            def _():
+                recv(step, k, q)
+                place(placed_theirs.at[i - 1], step, k, q, at)
+
+        add(picks_theirs.at[i - 1], placed_theirs.at[i - 1])
 
     for other in range(depths):
 
@@ -668,9 +703,9 @@
             rest = [q for q in range(slots) if not own_strip(k, q)]
             if rest:
                 whole = parts[k].at[slots - len(rest) :]
-                pltpu.make_async_copy(whole, whole, film_send.at[k]).wait()
+                pltpu.make_async_copy(whole, whole, film_send.at[kind(k)]).wait()
                 for step in range(1, depths):
-                    pltpu.make_async_copy(whole, whole, mix_send.at[k, step - 1]).wait()
+                    pltpu.make_async_copy(whole, whole, mix_send.at[kind(k), step - 1]).wait()
 
     def drain(lane, quota, home, local):
         for k in range(REACHES):
@@ -698,8 +733,8 @@
 
                 @pl.when(d != other)
                 def _():
-                    whole = windows.at[:, k, 0:half]
-                    pltpu.make_async_copy(whole, whole, pass_send.at[k, other]).wait()
+                    whole = windows.at[:, kind(k), 0:half]
+                    pltpu.make_async_copy(whole, whole, pass_send.at[kind(k), seat(other)]).wait()
 
 
 def body(sizes_of, crystal, probe, amplitude, shear, scan_x, scan_y, slot_angle, owner_slot, counts):
@@ -709,7 +744,10 @@
     half = slots // depths
     share = WX // angle_devs
     reach = share + SHEAR
-    depth_rows = -(-(slots * reach) // 128) * 128
+    kinds = bands(strips)
+    seats = 1 if depths == 2 else depths
+    local_rows = -(-(slots * reach) // 128) * 128
+    batch_rows = -(-(half * len(batch_of(strips, angle_devs)) * reach) // 128) * 128
     dft = dft_tables()
     bf16 = jnp.bfloat16
     scan_x, scan_y, slot_angle, owner_slot = [
@@ -736,29 +774,33 @@
     scratch += [
         pltpu.VMEM((depths, half, FRAME // depths, FRAME), bf16),
         pltpu.VMEM((half, REACHES, angle_devs, reach, 2 * FRAME), bf16),
-        pltpu.VMEM((angle_devs, REACHES, slots, reach, 2 * FRAME), bf16),
+        pltpu.VMEM((angle_devs, kinds, slots, reach, 2 * FRAME), bf16),
         pltpu.VMEM((half,) + dft.shape, bf16),
         pltpu.VMEM((half,) + probe.shape, bf16),
-        pltpu.VMEM((angle_devs, REACHES, layers * share, depth_rows), bf16),
-        pltpu.VMEM((depth_rows, 2 * columns), bf16),
+        pltpu.VMEM((layers * share, local_rows), bf16),
+        pltpu.VMEM((layers * share, batch_rows), bf16),
+        pltpu.VMEM((depths - 1, layers * share, batch_rows), bf16),
+        pltpu.VMEM((local_rows, 2 * columns), bf16),
+        pltpu.VMEM((batch_rows, 2 * columns), bf16),
+        pltpu.VMEM((depths - 1, batch_rows, 2 * columns), bf16),
         pltpu.VMEM((2 * FRAME, FRAME), jnp.float32),
         pltpu.VMEM((FRAME, 2 * FRAME), bf16),
         dma((3,)),
-        dma((REACHES,)),
+        dma((kinds,)),
         dma((REACHES, half)),
-        dma((REACHES, depths - 1)),
-        dma((REACHES, slots, depths - 1)),
-        dma((slots,)),
-        dma((depths, half)),
-        dma((depths,)),
+        dma((kinds, depths - 1)),
+        dma((kinds, slots, depths - 1)),
+        dma((half, seats)),
+        dma((half, seats)),
+        dma((seats,)),
         dma((1,)),
         dma((len(small),)),
         dma((angle_devs - 1, len(tables))),
         dma((angle_devs - 1, len(tables))),
         dma((angle_devs - 1, len(tables))),
         dma((REACHES, half)),
-        dma((REACHES, depths)),
-        dma((angle_devs, REACHES, slots)),
+        dma((kinds, seats)),
+        dma((angle_devs, kinds, slots)),
     ]
     scaling = 1.0 / (shear.shape[0] * angle_devs)
     result, *_ = pl.pallas_call(

time: 19.7 us -> 18.6 us (0.944)
  Pallas kernels: 18.6 us -> 17.5 us
    pallas_call x1, Pallas kernels: 18.6 us -> 17.5 us  [body(): pl.pallas_call(functools.partial(kernel, sizes, scaling), out_shape=(jax....]
where the time goes in v3:
time: 18.6 us; the launch traced here: 18.4 us
  Pallas kernels  17.5 us (94%)
  local copies, waits for them, and re-layouts  0.88 us (5%)
    pallas_call x1, Pallas kernels, body(): pl.pallas_call(functools.partial(kernel, sizes, scaling), out_shape=(jax....  17.5 us
    unnamed x1, local copies, waits for them, and re-layouts  0.88 us

profile of v3, /device:TPU:9, one launch (start us, length us, event | category | flops | bytes accessed | tf_op | source)
XLA Modules:
  0.0 18.4 jit_solution(15327749282657241715)
XLA Ops:
  0.0 17.5 %shard_map.100 = (f32[4,2,64,384]{3,2,1,0:T(8,128)S(1)}, s32[2,4,4]{2,1,0:T(4,128)}, s32[2,1,2,4]{3,2,1,0:T(2,128)}, s32[2,1,2,4]{3,2,1,0:T(2,128)}, s32[2,1,2,4]{3,2,1,0:T(2,128)}) custom-call(bf16[4,2,128,384]{3,2,1,0:T(8,128)(2,1)} %crystal.1, bf16[2,256,256]{2,1,0:T(8,128)(2,1)} %probe_in.1, bf16[2,128,256]{2,1,0:T(8,128)(2,1)} %amplitude.1, ...), custom_call_target="tpu_custom_call" | custom-call | tf_op jit(solution)/shard_map/pallas_call | solution.py:806
  17.5 0.9 %copy.12 = f32[4,2,64,384]{3,2,1,0:T(8,128)} copy(f32[4,2,64,384]{3,2,1,0:T(8,128)S(1)} %get-tuple-element.6) | data formatting | bytes 1572864

commit v4 on v3

--- a/solution.py
+++ b/solution.py
@@ -87,19 +87,12 @@
     counts_in,
     out,
     shear_out,
-    scan_y_out,
-    slot_angle_out,
-    owner_slot_out,
+    items_out,
     shear,
-    scan_x,
-    scan_y,
-    slot_angle,
-    owner_slot,
+    items,
     counts,
     shears,
-    scans_y,
-    slot_angles,
-    owner_slots,
+    others,
     film,
     probe,
     dft,
@@ -158,6 +151,7 @@
     s = lax.axis_index("strip")
     a = lax.axis_index("angle")
     d = lax.axis_index("depth")
+    scan_x, owner_slot, scan_y, slot_angle = [items.at[i] for i in range(4)]
     meta = Meta(shear, owner_slot, slots, ())
     margin = columns - FRAME
     kinds = bands(strips)
@@ -182,19 +176,12 @@
     def wrap(strip):
         return lax.rem(strip + 4 * strips, strips)
 
+    same = (scan_x_in, owner_slot_in, scan_y_in, slot_angle_in)
     metas = [
-        pltpu.make_async_copy(source, target, meta_load.at[i])
-        for i, (source, target) in enumerate(
-            (
-                (shear_in, shear),
-                (scan_x_in, scan_x),
-                (scan_y_in, scan_y),
-                (slot_angle_in, slot_angle),
-                (owner_slot_in, owner_slot),
-                (counts_in, counts),
-            )
-        )
+        pltpu.make_async_copy(shear_in, shear, meta_load.at[0]),
+        pltpu.make_async_copy(counts_in, counts, meta_load.at[1]),
     ]
+    several = [pltpu.make_async_copy(x, items.at[i], meta_load.at[2]) for i, x in enumerate(same)]
     loads = [
         pltpu.make_async_copy(
             crystal.at[:, part],
@@ -208,8 +195,12 @@
         for i, (source, target) in enumerate(((probe_in, probe), (tables_in, dft)))
     ]
     table, table_t = dft.at[0], dft.at[1]
-    for copy in metas + loads:
+    for copy in metas + several + loads:
         copy.start()
+
+    blank = jnp.zeros(windows.shape[:3] + (SHEAR, 2 * FRAME), jnp.bfloat16)
+    windows[:, :, :, 0:SHEAR] = blank
+    windows[:, :, :, share:reach] = blank
 
     barrier = pltpu.get_barrier_semaphore()
     shifts = set()
@@ -242,6 +233,7 @@
 
     for copy in metas:
         copy.wait()
+    pltpu.make_async_copy(items, items, meta_load.at[2]).wait()
     pltpu.make_async_copy(film, film, load_sem.at[0]).wait()
     for copy in late:
         copy.start()
@@ -350,29 +342,27 @@
             amplitude.at[other * half : (other + 1) * half], measured.at[d], amp_recv.at[0]
         )
 
-    tables = (
-        (shear_in, shear_out, shears),
-        (scan_y_in, scan_y_out, scans_y),
-        (slot_angle_in, slot_angle_out, slot_angles),
-        (owner_slot_in, owner_slot_out, owner_slots),
-    )
-
     def meta_copies(step):
-        return [
-            rcopy(
+        def send(source, target, i):
+            return rcopy(
                 source,
-                target.at[step],
+                target,
                 meta_send.at[step - 1, i],
                 meta_recv.at[step - 1, i],
                 angle=lax.rem(a + step, angle_devs),
             )
-            for i, (source, target, _) in enumerate(tables)
-        ]
+
+        first = [send(shear_in, shear_out.at[step], 0)]
+        return first + [send(x, items_out.at[step, i], 1) for i, x in enumerate(same[1:])]
+
+    def meta_waits(step, sem):
+        for i, ref in enumerate((shear_out.at[step], items_out.at[step])):
+            pltpu.make_async_copy(ref, ref, sem.at[step - 1, i]).wait()
 
     def meta_pulls(step):
         return [
-            pltpu.make_async_copy(target.at[step], local.at[step], meta_pull.at[step - 1, i])
-            for i, (_, target, local) in enumerate(tables)
+            pltpu.make_async_copy(shear_out.at[step], shears.at[step], meta_pull.at[step - 1, 0]),
+            pltpu.make_async_copy(items_out.at[step], others.at[step], meta_pull.at[step - 1, 1]),
         ]
 
     for step in range(1, angle_devs):
@@ -418,8 +408,8 @@
 
     groups = [(meta, scan_y, slot_angle)]
     for step in range(1, angle_devs):
-        lead = (step,)
-        groups.append((Meta(shears, owner_slots, slots, lead), scans_y, slot_angles))
+        owner_slots, scans_y, slot_angles = [others.at[step, i] for i in range(3)]
+        groups.append((Meta(shears.at[step], owner_slots, slots, ()), scans_y, slot_angles))
 
     def prepare(target, items):
         wanted = []
@@ -454,12 +444,20 @@
     pltpu.make_async_copy(measured, measured, amp_recv.at[0]).wait()
 
 
+    def edge(k, part):
+        return (k == 0 and part == 0) or (k == 2 and part == angle_devs - 1)
+
+    def filled(k, narrow):
+        low = SHEAR if narrow and k == 0 else 0
+        return slice(low, low + (share if narrow else reach))
+
     def cut_copy(k, lane, quota, home, part):
         step = lax.rem(part - a + angle_devs, angle_devs)
+        narrow = edge(k, part)
         return rcopy(
-            cuts.at[lane, k, part],
-            windows.at[step, kind(k), quota],
-            cut_send.at[k, lane],
+            cuts.at[lane, k, part, filled(k, narrow)],
+            windows.at[step, kind(k), quota, filled(k, narrow)],
+            cut_send.at[REACHES + k // 2 if narrow else k, lane],
             win_recv.at[step, kind(k), quota],
             strip=wrap(home + k),
             angle=part,
@@ -527,13 +525,13 @@
         arrive(2)
         spectrum = spec[...] + forward(WX, FRAME, got2[lane])
         spec_re, spec_im = spectrum[:FRAME], spectrum[FRAME:]
-        magnitude = jnp.sqrt(spec_re * spec_re + spec_im * spec_im)
+        power = spec_re * spec_re + spec_im * spec_im
         levels = jnp.concatenate(
             [measured[source, lane] for source in range(depths)], axis=0
         ).astype(jnp.float32)
         live = meta.slot(home, quota) < counts[0, home]
         live = jnp.where(live, 1.0, 0.0).astype(jnp.float32)
-        factor = (1.0 - levels / jnp.maximum(magnitude, 1.0)) * live
+        factor = (1.0 - levels * lax.rsqrt(jnp.maximum(power, 1.0))) * live
         residual = jnp.concatenate([spec_re * factor, spec_im * factor], axis=1).astype(
             jnp.bfloat16
         )
@@ -585,8 +583,7 @@
     owned(work)
 
     for step in range(1, angle_devs):
-        for copy in meta_copies(step):
-            copy.wait_recv()
+        meta_waits(step, meta_recv)
         for copy in meta_pulls(step):
             copy.start()
     for step in range(1, angle_devs):
@@ -599,29 +596,47 @@
         prepare(picks_theirs.at[step - 1], theirs[step - 1])
 
 
-    def pass_copy(step, k, q, other):
-        return rcopy(
-            windows.at[step, kind(k), q],
-            windows.at[step, kind(k), q],
-            pass_send.at[kind(k), seat(other)],
-            win_recv.at[step, kind(k), q],
-            depth=other,
-        )
+    def sized(k, act):
+        if k == 1:
+            act(filled(k, False))
+        else:
+            narrow = a == (0 if k == 0 else angle_devs - 1)
+
+            @pl.when(narrow)
+            def _():
+                act(filled(k, True))
+
+            @pl.when(jnp.logical_not(narrow))
+            def _():
+                act(filled(k, False))
 
     def recv(step, k, q):
-        window = windows.at[step, kind(k), q]
-        pltpu.make_async_copy(window, window, win_recv.at[step, kind(k), q]).wait()
+        def act(rows):
+            window = windows.at[step, kind(k), q, rows]
+            pltpu.make_async_copy(window, window, win_recv.at[step, kind(k), q]).wait()
+
+        sized(k, act)
 
     def relay(step, k):
         for q in range(slots):
 
             @pl.when(d == q // half)
             def _():
-                if not (step == 0 and own_strip(k, q)):
-                    recv(step, k, q)
-                for other in range(depths):
-                    if other != q // half:
-                        pass_copy(step, k, q, other).start()
+                def act(rows):
+                    window = windows.at[step, kind(k), q, rows]
+                    if not (step == 0 and own_strip(k, q)):
+                        pltpu.make_async_copy(window, window, win_recv.at[step, kind(k), q]).wait()
+                    for other in range(depths):
+                        if other != q // half:
+                            rcopy(
+                                window,
+                                window,
+                                pass_send.at[kind(k), seat(other)],
+                                win_recv.at[step, kind(k), q],
+                                depth=other,
+                            ).start()
+
+                sized(k, act)
 
     def place(target, step, k, q, at):
         source, corners, _ = groups[step]
@@ -654,7 +669,7 @@
 
             @pl.when(d != q // half)
             def _():
-                pass_copy(0, 1, q, q // half).wait_recv()
+                recv(0, 1, q)
 
         for item in locals_:
             place(placed_local, *item)
@@ -688,8 +703,7 @@
             amp_copy(other).wait_send()
 
     for step in range(1, angle_devs):
-        for copy in meta_copies(step):
-            copy.wait_send()
+        meta_waits(step, meta_send)
     for k in range(REACHES):
 
         @pl.when(reached(k))
@@ -710,7 +724,13 @@
     def drain(lane, quota, home, local):
         for k in range(REACHES):
             whole = cuts.at[lane, k]
-            if k == 1:
+            if k != 1:
+                narrow = cuts.at[lane, k, 0, 0:share]
+                pltpu.make_async_copy(narrow, narrow, cut_send.at[REACHES + k // 2, lane]).wait()
+                if angle_devs > 1:
+                    most = cuts.at[lane, k, 1:]
+                    pltpu.make_async_copy(most, most, cut_send.at[k, lane]).wait()
+            else:
                 most = cuts.at[lane, k, 1:]
 
                 @pl.when(local)
@@ -720,8 +740,6 @@
                 @pl.when(jnp.logical_not(local))
                 def _():
                     pltpu.make_async_copy(whole, whole, cut_send.at[k, lane]).wait()
-            else:
-                pltpu.make_async_copy(whole, whole, cut_send.at[k, lane]).wait()
 
     owned(drain)
 
@@ -733,8 +751,13 @@
 
                 @pl.when(d != other)
                 def _():
-                    whole = windows.at[:, kind(k), 0:half]
-                    pltpu.make_async_copy(whole, whole, pass_send.at[kind(k), seat(other)]).wait()
+                    def act(rows):
+                        whole = windows.at[:, kind(k), 0:half, rows]
+                        pltpu.make_async_copy(
+                            whole, whole, pass_send.at[kind(k), seat(other)]
+                        ).wait()
+
+                    sized(k, act)
 
 
 def body(sizes_of, crystal, probe, amplitude, shear, scan_x, scan_y, slot_angle, owner_slot, counts):
@@ -754,13 +777,13 @@
         jnp.swapaxes(value, 1, 2) for value in (scan_x, scan_y, slot_angle, owner_slot)
     ]
     sizes = (strips, angle_devs, depths, layers, slots, columns)
-    tables = (shear, scan_y, slot_angle, owner_slot)
     hbm = pl.BlockSpec(memory_space=pltpu.HBM)
     vmem = pl.BlockSpec(memory_space=pltpu.VMEM)
     dma = pltpu.SemaphoreType.DMA
     small = (shear, scan_x, scan_y, slot_angle, owner_slot, counts)
-    scratch = [pltpu.SMEM(x.shape, jnp.int32) for x in small]
-    scratch += [pltpu.SMEM((angle_devs,) + x.shape, jnp.int32) for x in tables]
+    gathered = ((angle_devs,) + shear.shape, (angle_devs, 3) + scan_x.shape)
+    scratch = [pltpu.SMEM(x, jnp.int32) for x in (shear.shape, (4,) + scan_x.shape, counts.shape)]
+    scratch += [pltpu.SMEM(x, jnp.int32) for x in gathered]
     scratch += [
         pltpu.VMEM((layers, WX, 2 * columns), bf16),
         pltpu.VMEM(probe.shape, bf16),
@@ -794,11 +817,11 @@
         dma((half, seats)),
         dma((seats,)),
         dma((1,)),
-        dma((len(small),)),
-        dma((angle_devs - 1, len(tables))),
-        dma((angle_devs - 1, len(tables))),
-        dma((angle_devs - 1, len(tables))),
-        dma((REACHES, half)),
+        dma((3,)),
+        dma((angle_devs - 1, 2)),
+        dma((angle_devs - 1, 2)),
+        dma((angle_devs - 1, 2)),
+        dma((REACHES + 2, half)),
         dma((kinds, seats)),
         dma((angle_devs, kinds, slots)),
     ]
@@ -806,9 +829,9 @@
     result, *_ = pl.pallas_call(
         functools.partial(kernel, sizes, scaling),
         out_shape=(jax.ShapeDtypeStruct((layers, 2, share, columns), jnp.float32),)
-        + tuple(jax.ShapeDtypeStruct((angle_devs,) + x.shape, jnp.int32) for x in tables),
+        + tuple(jax.ShapeDtypeStruct(x, jnp.int32) for x in gathered),
         in_specs=[hbm] * 10,
-        out_specs=(vmem,) + (hbm,) * 4,
+        out_specs=(vmem,) + (hbm,) * 2,
         scratch_shapes=scratch,
         compiler_params=pltpu.CompilerParams(
             collective_id=0, has_side_effects=True, vmem_limit_bytes=VMEM_LIMIT

time: 18.6 us -> 18.2 us (0.978)
  Pallas kernels: 17.5 us -> 17 us
    pallas_call x1, Pallas kernels: 17.5 us -> 17 us  [body(): pl.pallas_call(functools.partial(kernel, sizes, scaling), out_shape=(jax....]
where the time goes in v4:
time: 18.2 us; the launch traced here: 17.9 us
  Pallas kernels  17 us (93%)
  local copies, waits for them, and re-layouts  0.88 us (5%)
    pallas_call x1, Pallas kernels, body(): pl.pallas_call(functools.partial(kernel, sizes, scaling), out_shape=(jax....  17 us
    unnamed x1, local copies, waits for them, and re-layouts  0.88 us

profile of v4, /device:TPU:9, one launch (start us, length us, event | category | flops | bytes accessed | tf_op | source)
XLA Modules:
  0.0 17.9 jit_solution(16770869024652710761)
XLA Ops:
  0.0 17.0 %shard_map.100 = (f32[4,2,64,384]{3,2,1,0:T(8,128)S(1)}, s32[2,4,4]{2,1,0:T(4,128)}, s32[2,3,1,2,4]{4,3,2,1,0:T(2,128)}) custom-call(bf16[4,2,128,384]{3,2,1,0:T(8,128)(2,1)} %crystal.1, bf16[2,256,256]{2,1,0:T(8,128)(2,1)} %probe_in.1, bf16[2,128,256]{2,1,0:T(8,128)(2,1)} %amplitude.1, bf16[2,512,512]{2,1,0:T(8,128)(2,1)} %constant.2.clone.tables_in, ...), custom_call_target="tpu_custom_call" | custom-call | tf_op jit(solution)/shard_map/pallas_call | solution.py:829
  17.0 0.9 %copy.12 = f32[4,2,64,384]{3,2,1,0:T(8,128)} copy(f32[4,2,64,384]{3,2,1,0:T(8,128)S(1)} %get-tuple-element.6) | data formatting | bytes 1572864

commit v5 on v4

--- a/solution.py
+++ b/solution.py
@@ -14,6 +14,7 @@
 REACHES = 3
 ROWS = (WX, FRAME, FRAME - WX)
 BASES = (0, 0, WX)
+EARLY = 32
 VMEM_LIMIT = 44 * 2**20
 MESH = pl.DeviceIdType.MESH
 
@@ -123,6 +124,7 @@
     spec,
     back,
     load_sem,
+    early_send,
     film_send,
     film_recv,
     mix_send,
@@ -238,28 +240,49 @@
     for copy in late:
         copy.start()
 
-    def block(k, device):
-        rows = ROWS[k] // depths
-        return pl.ds(pl.multiple_of(device * rows, rows), rows)
+    def ahead(k, q):
+        return k != 1 and q == 0
+
+    def size(k, q):
+        return (ROWS[k] - (EARLY if ahead(k, q) else 0)) // depths
+
+    def block(k, q, device):
+        rows = size(k, q)
+        low = EARLY if ahead(k, q) else 0
+        return pl.ds(pl.multiple_of(low + device * rows, 16), rows)
+
+    def crossing(k):
+        return 0 if quarter == 1 else kind(k)
 
     def mix_copy(k, q, step):
         target = lax.rem(d + step, depths)
         return rcopy(
-            sent[k].at[q, block(k, target)],
-            mix[k].at[q, step - 1],
-            mix_send.at[kind(k), step - 1],
-            mix_recv.at[kind(k), q, step - 1],
+            sent[k].at[q, block(k, q, target)],
+            mix[k].at[q, step - 1, 0 : size(k, q)],
+            early_send.at[kind(k)] if ahead(k, q) else mix_send.at[crossing(k), step - 1],
+            mix_recv.at[crossing(k), q, step - 1],
             depth=target,
         )
 
     def film_copy(k, q):
         return rcopy(
-            parts[k].at[q],
-            got[k].at[q % half, block(k, d)],
-            film_send.at[kind(k)],
+            parts[k].at[q, 0 : size(k, q)],
+            got[k].at[q % half, block(k, q, d)],
+            early_send.at[kind(k)] if ahead(k, q) else film_send.at[crossing(k)],
             film_recv.at[k, q % half],
             strip=wrap(s - k + 4 * (q % quarter) + 1),
             depth=q // half,
+        )
+
+    def early_copy(k):
+        low = jnp.where(d == 0, 0, ROWS[k] + (d - 1) * EARLY)
+        return rcopy(
+            sent[k].at[0, 0:EARLY],
+            got[k].at[0, pl.ds(pl.multiple_of(low, 16), EARLY)],
+            early_send.at[kind(k)],
+            film_recv.at[k, 0],
+            strip=wrap(s - k + 1),
+            depth=0,
         )
 
     def own_copy(q):
@@ -276,11 +299,12 @@
             mix_copy(k, q, step).start()
 
     def merge(k, q):
-        value = sent[k][q, block(k, d)].astype(jnp.float32)
+        rows = size(k, q)
+        value = sent[k][q, block(k, q, d)].astype(jnp.float32)
         for step in range(1, depths):
             mix_copy(k, q, step).wait_recv()
-            value = value + mix[k][q, step - 1].astype(jnp.float32)
-        parts[k][q] = value.astype(jnp.bfloat16)
+            value = value + mix[k][q, step - 1, 0:rows].astype(jnp.float32)
+        parts[k][q, 0:rows] = value.astype(jnp.bfloat16)
         film_copy(k, q).start()
 
     def own_strip(k, q):
@@ -324,7 +348,9 @@
 
         @pl.when(reached(k))
         def _():
-            for q in range(slots):
+            exchange(k, 0)
+            early_copy(k).start()
+            for q in range(1, slots):
                 exchange(k, q)
 
 
@@ -474,7 +500,24 @@
 
     def work(lane, quota, home, local):
         def arrive(k):
-            pltpu.make_async_copy(got[k].at[lane], got[k].at[lane], film_recv.at[k, lane]).wait()
+            whole = got[k].at[lane, 0 : ROWS[k]]
+            if lane or k == 1:
+                pltpu.make_async_copy(whole, whole, film_recv.at[k, lane]).wait()
+            else:
+
+                @pl.when(quota == 0)
+                def _():
+                    full = got[k].at[lane]
+                    pltpu.make_async_copy(full, full, film_recv.at[k, lane]).wait()
+                    value = got[k][lane, 0:EARLY].astype(jnp.float32)
+                    for source in range(1, depths):
+                        low = ROWS[k] + (source - 1) * EARLY
+                        value = value + got[k][lane, low : low + EARLY].astype(jnp.float32)
+                    got[k][lane, 0:EARLY] = value.astype(jnp.bfloat16)
+
+                @pl.when(quota != 0)
+                def _():
+                    pltpu.make_async_copy(whole, whole, film_recv.at[k, lane]).wait()
 
         corner = meta.pick(scan_y, home, quota)
         gap = differences(FRAME, FRAME)
@@ -521,9 +564,9 @@
             return dot(left, jnp.concatenate([section[:, :FRAME], section[:, FRAME:]], axis=0))
 
         arrive(0)
-        spec[...] = forward(0, WX, got0[lane])
+        spec[...] = forward(0, WX, got0[lane, 0:WX])
         arrive(2)
-        spectrum = spec[...] + forward(WX, FRAME, got2[lane])
+        spectrum = spec[...] + forward(WX, FRAME, got2[lane, 0 : FRAME - WX])
         spec_re, spec_im = spectrum[:FRAME], spectrum[FRAME:]
         power = spec_re * spec_re + spec_im * spec_im
         levels = jnp.concatenate(
@@ -715,11 +758,15 @@
                     def _():
                         own_copy(q).wait_send()
             rest = [q for q in range(slots) if not own_strip(k, q)]
+            if ahead(k, 0):
+                first = sent[k].at[0]
+                pltpu.make_async_copy(first, first, early_send.at[kind(k)]).wait()
+                rest = rest[1:]
             if rest:
                 whole = parts[k].at[slots - len(rest) :]
-                pltpu.make_async_copy(whole, whole, film_send.at[kind(k)]).wait()
+                pltpu.make_async_copy(whole, whole, film_send.at[crossing(k)]).wait()
                 for step in range(1, depths):
-                    pltpu.make_async_copy(whole, whole, mix_send.at[kind(k), step - 1]).wait()
+                    pltpu.make_async_copy(whole, whole, mix_send.at[crossing(k), step - 1]).wait()
 
     def drain(lane, quota, home, local):
         for k in range(REACHES):
@@ -769,6 +816,7 @@
     reach = share + SHEAR
     kinds = bands(strips)
     seats = 1 if depths == 2 else depths
+    crossings = 1 if strips == 4 else kinds
     local_rows = -(-(slots * reach) // 128) * 128
     batch_rows = -(-(half * len(batch_of(strips, angle_devs)) * reach) // 128) * 128
     dft = dft_tables()
@@ -790,7 +838,11 @@
         pltpu.VMEM(dft.shape, bf16),
     ]
     scratch += [pltpu.VMEM((slots, rows, 2 * FRAME), bf16) for rows in ROWS]
-    scratch += [pltpu.VMEM((half, rows, 2 * FRAME), bf16) for rows in ROWS]
+    extra = (depths - 1) * EARLY
+    scratch += [
+        pltpu.VMEM((half, rows + (0 if k == 1 else extra), 2 * FRAME), bf16)
+        for k, rows in enumerate(ROWS)
+    ]
     scratch += [pltpu.VMEM((slots, depths - 1, rows // depths, 2 * FRAME), bf16) for rows in ROWS]
     scratch += [pltpu.VMEM((slots, rows // depths, 2 * FRAME), bf16) for rows in ROWS]
     scratch += [pltpu.VMEM((depths, half, FRAME, 2 * FRAME), bf16)]
@@ -810,9 +862,10 @@
         pltpu.VMEM((FRAME, 2 * FRAME), bf16),
         dma((3,)),
         dma((kinds,)),
+        dma((crossings,)),
         dma((REACHES, half)),
-        dma((kinds, depths - 1)),
-        dma((kinds, slots, depths - 1)),
+        dma((crossings, depths - 1)),
+        dma((crossings, slots, depths - 1)),
         dma((half, seats)),
         dma((half, seats)),
         dma((seats,)),

time: 18.2 us -> 17.8 us (0.978)
  Pallas kernels: 17 us -> 16.6 us
    pallas_call x1, Pallas kernels: 17 us -> 16.6 us  [body(): pl.pallas_call(functools.partial(kernel, sizes, scaling), out_shape=(jax....]
where the time goes in v5:
time: 17.8 us; the launch traced here: 17.5 us
  Pallas kernels  16.6 us (93%)
  local copies, waits for them, and re-layouts  0.88 us (5%)
    pallas_call x1, Pallas kernels, body(): pl.pallas_call(functools.partial(kernel, sizes, scaling), out_shape=(jax....  16.6 us
    unnamed x1, local copies, waits for them, and re-layouts  0.88 us

profile of v5, /device:TPU:9, one launch (start us, length us, event | category | flops | bytes accessed | tf_op | source)
XLA Modules:
  0.0 17.5 jit_solution(9236769754612678739)
XLA Ops:
  0.0 16.6 %shard_map.100 = (f32[4,2,64,384]{3,2,1,0:T(8,128)S(1)}, s32[2,4,4]{2,1,0:T(4,128)}, s32[2,3,1,2,4]{4,3,2,1,0:T(2,128)}) custom-call(bf16[4,2,128,384]{3,2,1,0:T(8,128)(2,1)} %crystal.1, bf16[2,256,256]{2,1,0:T(8,128)(2,1)} %probe_in.1, bf16[2,128,256]{2,1,0:T(8,128)(2,1)} %amplitude.1, bf16[2,512,512]{2,1,0:T(8,128)(2,1)} %constant.2.clone.tables_in, ...), custom_call_target="tpu_custom_call" | custom-call | tf_op jit(solution)/shard_map/pallas_call | solution.py:882
  16.7 0.9 %copy.12 = f32[4,2,64,384]{3,2,1,0:T(8,128)} copy(f32[4,2,64,384]{3,2,1,0:T(8,128)S(1)} %get-tuple-element.6) | data formatting | bytes 1572864

commit v6 on v5

--- a/solution.py
+++ b/solution.py
@@ -115,6 +115,7 @@
     windows,
     dft_rot,
     probe_rot,
+    inner,
     picks_local,
     picks_mine,
     picks_theirs,
@@ -160,8 +161,14 @@
     batch = batch_of(strips, angle_devs)
     rows_of = dict(zip(batch, range(len(batch))))
 
+    outer = strips - 3
+    spread = (1, None) if kinds == 2 else (1, 0, 2)
+
     def kind(k):
-        return k % kinds
+        return 0 if k is None else k % kinds
+
+    def home_of(k):
+        return jnp.where(s <= outer, s, s - 2) if k is None else s - k
 
     def seat(device):
         return 0 if depths == 2 else device
@@ -335,7 +342,13 @@
             sent[k][q] = jnp.concatenate(wound, axis=1).astype(jnp.bfloat16)
 
     def reached(k):
-        return (s - k >= 0) & (s - k <= strips - 3)
+        return (s - k >= 0) & (s - k <= outer)
+
+    def guarded(k, act):
+        if k is None:
+            act()
+        else:
+            pl.when(reached(k))(act)
 
     for k in (0, 2):
 
@@ -440,10 +453,18 @@
     def prepare(target, items):
         wanted = []
         for step, k, q, at in items:
-            home = jnp.clip(s - k, 0, strips - 1)
-            source, _, angles = groups[step]
+            home = jnp.clip(home_of(k), 0, strips - 1)
+            source, corners, angles = groups[step]
+
+            def fill():
+                first = lanes(reach) >= source.pick(corners, home, q)
+                inner[step, kind(k), q] = one_hot(first)
+
+            guarded(k, fill)
             angle = source.pick(angles, home, q)
-            base = jnp.where(reached(k), at + SHEAR, -4 * target.shape[1])
+            base = at + SHEAR
+            if k is not None:
+                base = jnp.where(reached(k), base, -4 * target.shape[1])
             wanted.append([base - source.shear(angle, z) for z in range(layers)])
         gap = differences(share, target.shape[1])
         for z in range(layers):
@@ -459,7 +480,7 @@
             (step, k, depth * half + lane, (lane * len(batch) + rows_of[step, kind(k)]) * reach)
             for lane in range(half)
             for step in list(range(1, angle_devs)) + [0]
-            for k in (1, 0, 2)
+            for k in spread
             if (step, k) != (0, 1)
         ]
 
@@ -476,6 +497,11 @@
     def filled(k, narrow):
         low = SHEAR if narrow and k == 0 else 0
         return slice(low, low + (share if narrow else reach))
+
+    def cut_sem(k, narrow, lane, part):
+        if k == 1 and quarter > 1:
+            return cut_send.at[2, lane]
+        return cut_send.at[1 if narrow else 0, lane]
 
     def cut_copy(k, lane, quota, home, part):
         step = lax.rem(part - a + angle_devs, angle_devs)
@@ -483,7 +509,7 @@
         return rcopy(
             cuts.at[lane, k, part, filled(k, narrow)],
             windows.at[step, kind(k), quota, filled(k, narrow)],
-            cut_send.at[REACHES + k // 2 if narrow else k, lane],
+            cut_sem(k, narrow, lane, part),
             win_recv.at[step, kind(k), quota],
             strip=wrap(home + k),
             angle=part,
@@ -593,14 +619,13 @@
                 [probe_re * re + probe_im * im, probe_re * im - probe_im * re], axis=1
             ).astype(jnp.bfloat16)
 
-        def cut(k, part, low, value):
+        def send(k, low, value):
             gap = differences(reach, value.shape[0])
-            first = WX * k - offset + part * share - SHEAR - low
-            cuts[lane, k, part] = dot(one_hot(gap == first), value).astype(jnp.bfloat16)
-
-        def send(k, low, value):
+            first = WX * k - offset - SHEAR - low
+            chosen = [one_hot(gap == first + part * share) for part in range(angle_devs)]
+            pieces = dot(jnp.concatenate(chosen, axis=0), value).astype(jnp.bfloat16)
             for part in range(angle_devs):
-                cut(k, part, low, value)
+                cuts[lane, k, part] = pieces[part * reach : (part + 1) * reach]
                 copy = cut_copy(k, lane, quota, home, part)
                 if k == 1:
 
@@ -658,7 +683,18 @@
             window = windows.at[step, kind(k), q, rows]
             pltpu.make_async_copy(window, window, win_recv.at[step, kind(k), q]).wait()
 
-        sized(k, act)
+        if k is None:
+            narrow = a == jnp.where(s <= outer, 0, angle_devs - 1)
+
+            @pl.when(narrow)
+            def _():
+                act(slice(0, share))
+
+            @pl.when(jnp.logical_not(narrow))
+            def _():
+                act(slice(0, reach))
+        else:
+            sized(k, act)
 
     def relay(step, k):
         for q in range(slots):
@@ -682,20 +718,18 @@
                 sized(k, act)
 
     def place(target, step, k, q, at):
-        source, corners, _ = groups[step]
-        first = lanes(reach) >= source.pick(corners, s - k, q)
+        inside = inner[step, kind(k), q]
         window = windows.at[step, kind(k), q]
         rows = slice(at, at + reach)
         for part in range(2):
-            head = window[:, part * FRAME : part * FRAME + margin].astype(jnp.float32)
+            head = window[:, part * FRAME : part * FRAME + margin]
+            kept = head * inside
             left = part * columns
-            target[rows, left : left + margin] = jnp.where(first, head, 0.0).astype(jnp.bfloat16)
+            target[rows, left : left + margin] = kept
             target[rows, left + margin : left + FRAME] = window[
                 :, part * FRAME + margin : (part + 1) * FRAME
             ]
-            target[rows, left + FRAME : left + columns] = jnp.where(first, 0.0, head).astype(
-                jnp.bfloat16
-            )
+            target[rows, left + FRAME : left + columns] = head - kept
 
     def add(chosen, target):
         value = dot(chosen[...], target[...]) * scaling
@@ -718,24 +752,30 @@
             place(placed_local, *item)
         add(picks_local, placed_local)
 
-    for step, k in [(step, k) for step in list(range(1, angle_devs)) + [0] for k in (1, 0, 2)]:
+    for k, step in [(k, step) for k in range(REACHES) for step in range(angle_devs)]:
         if (step, k) != (0, 1):
 
             @pl.when(reached(k))
             def _():
                 relay(step, k)
-                for item in mine:
-                    if item[:2] == (step, k):
-                        place(placed_mine, *item)
+
+    for item in sorted(mine, key=lambda item: item[1] is None):
+        guarded(item[1], lambda: place(placed_mine, *item))
 
     add(picks_mine, placed_mine)
     for i in range(1, depths):
-        for step, k, q, at in theirs[i - 1]:
-
-            @pl.when(reached(k))
-            def _():
-                recv(step, k, q)
-                place(placed_theirs.at[i - 1], step, k, q, at)
+        held = sorted(theirs[i - 1], key=lambda item: item[1] is None)
+        for item in held:
+
+            def take():
+                recv(*item[:3])
+                if item[1] is not None:
+                    place(placed_theirs.at[i - 1], *item)
+
+            guarded(item[1], take)
+        for item in held:
+            if item[1] is None:
+                place(placed_theirs.at[i - 1], *item)
 
         add(picks_theirs.at[i - 1], placed_theirs.at[i - 1])
 
@@ -768,25 +808,26 @@
                 for step in range(1, depths):
                     pltpu.make_async_copy(whole, whole, mix_send.at[crossing(k), step - 1]).wait()
 
+    def finish(ref, sem):
+        pltpu.make_async_copy(ref, ref, sem).wait()
+
     def drain(lane, quota, home, local):
-        for k in range(REACHES):
-            whole = cuts.at[lane, k]
-            if k != 1:
-                narrow = cuts.at[lane, k, 0, 0:share]
-                pltpu.make_async_copy(narrow, narrow, cut_send.at[REACHES + k // 2, lane]).wait()
+        finish(cuts.at[lane, 0:2, 0, 0:share], cut_send.at[1, lane])
+        if quarter == 1:
+            if angle_devs > 1:
+                finish(cuts.at[lane, :, 1:], cut_send.at[0, lane])
+        else:
+            if angle_devs > 1:
+                finish(cuts.at[lane, 0:2, 1:], cut_send.at[0, lane])
+
+            @pl.when(local)
+            def _():
                 if angle_devs > 1:
-                    most = cuts.at[lane, k, 1:]
-                    pltpu.make_async_copy(most, most, cut_send.at[k, lane]).wait()
-            else:
-                most = cuts.at[lane, k, 1:]
-
-                @pl.when(local)
-                def _():
-                    pltpu.make_async_copy(most, most, cut_send.at[k, lane]).wait()
-
-                @pl.when(jnp.logical_not(local))
-                def _():
-                    pltpu.make_async_copy(whole, whole, cut_send.at[k, lane]).wait()
+                    finish(cuts.at[lane, 1, 1:], cut_send.at[2, lane])
+
+            @pl.when(jnp.logical_not(local))
+            def _():
+                finish(cuts.at[lane, 1], cut_send.at[2, lane])
 
     owned(drain)
 
@@ -852,6 +893,7 @@
         pltpu.VMEM((angle_devs, kinds, slots, reach, 2 * FRAME), bf16),
         pltpu.VMEM((half,) + dft.shape, bf16),
         pltpu.VMEM((half,) + probe.shape, bf16),
+        pltpu.VMEM((angle_devs, kinds, slots, reach, columns - FRAME), bf16),
         pltpu.VMEM((layers * share, local_rows), bf16),
         pltpu.VMEM((layers * share, batch_rows), bf16),
         pltpu.VMEM((depths - 1, layers * share, batch_rows), bf16),
@@ -874,7 +916,7 @@
         dma((angle_devs - 1, 2)),
         dma((angle_devs - 1, 2)),
         dma((angle_devs - 1, 2)),
-        dma((REACHES + 2, half)),
+        dma((2 if strips == 4 else 3, half)),
         dma((kinds, seats)),
         dma((angle_devs, kinds, slots)),
     ]

time: 17.8 us -> 17.6 us (0.989)
    pallas_call x1, Pallas kernels: 16.6 us -> 16.5 us  [body(): pl.pallas_call(functools.partial(kernel, sizes, scaling), out_shape=(jax....]
where the time goes in v6:
time: 17.6 us; the launch traced here: 17.3 us
  Pallas kernels  16.5 us (94%)
  local copies, waits for them, and re-layouts  0.88 us (5%)
    pallas_call x1, Pallas kernels, body(): pl.pallas_call(functools.partial(kernel, sizes, scaling), out_shape=(jax....  16.5 us
    unnamed x1, local copies, waits for them, and re-layouts  0.88 us

profile of v6, /device:TPU:9, one launch (start us, length us, event | category | flops | bytes accessed | tf_op | source)
XLA Modules:
  0.0 17.3 jit_solution(16152271472908509726)
XLA Ops:
  0.0 16.5 %shard_map.100 = (f32[4,2,64,384]{3,2,1,0:T(8,128)S(1)}, s32[2,4,4]{2,1,0:T(4,128)}, s32[2,3,1,2,4]{4,3,2,1,0:T(2,128)}) custom-call(bf16[4,2,128,384]{3,2,1,0:T(8,128)(2,1)} %crystal.1, bf16[2,256,256]{2,1,0:T(8,128)(2,1)} %probe_in.1, bf16[2,128,256]{2,1,0:T(8,128)(2,1)} %amplitude.1, bf16[2,512,512]{2,1,0:T(8,128)(2,1)} %constant.2.clone.tables_in, ...), custom_call_target="tpu_custom_call" | custom-call | tf_op jit(solution)/shard_map/pallas_call | solution.py:924
  16.5 0.9 %copy.12 = f32[4,2,64,384]{3,2,1,0:T(8,128)} copy(f32[4,2,64,384]{3,2,1,0:T(8,128)S(1)} %get-tuple-element.6) | data formatting | bytes 1572864

commit v7 on v6

--- a/solution.py
+++ b/solution.py
@@ -87,6 +87,8 @@
     owner_slot_in,
     counts_in,
     out,
+    picks_theirs,
+    placed_theirs,
     shear_out,
     items_out,
     shear,
@@ -118,10 +120,8 @@
     inner,
     picks_local,
     picks_mine,
-    picks_theirs,
     placed_local,
     placed_mine,
-    placed_theirs,
     spec,
     back,
     load_sem,
@@ -777,7 +777,6 @@
             if item[1] is None:
                 place(placed_theirs.at[i - 1], *item)
 
-        add(picks_theirs.at[i - 1], placed_theirs.at[i - 1])
 
     for other in range(depths):
 
@@ -846,6 +845,27 @@
                         ).wait()
 
                     sized(k, act)
+
+
+def finish_kernel(flushes, scaling, sums, picks, placed, out, total, sem):
+    layers, parts, share, columns = sums.shape
+    step = layers // flushes
+    copies = []
+    for i in range(flushes):
+        rows = slice(i * step * share, (i + 1) * step * share)
+        value = dot(picks[0, rows], placed[0])
+        for other in range(1, picks.shape[0]):
+            value = value + dot(picks[other, rows], placed[other])
+        value = value * scaling
+        for z in range(step):
+            for part in range(parts):
+                piece = value[z * share : (z + 1) * share, part * columns : (part + 1) * columns]
+                total[i * step + z, part] = sums[i * step + z, part] + piece
+        at = slice(i * step, (i + 1) * step)
+        copies.append(pltpu.make_async_copy(total.at[at], out.at[at], sem.at[i]))
+        copies[-1].start()
+    for copy in copies:
+        copy.wait()
 
 
 def body(sizes_of, crystal, probe, amplitude, shear, scan_x, scan_y, slot_angle, owner_slot, counts):
@@ -896,10 +916,8 @@
         pltpu.VMEM((angle_devs, kinds, slots, reach, columns - FRAME), bf16),
         pltpu.VMEM((layers * share, local_rows), bf16),
         pltpu.VMEM((layers * share, batch_rows), bf16),
-        pltpu.VMEM((depths - 1, layers * share, batch_rows), bf16),
         pltpu.VMEM((local_rows, 2 * columns), bf16),
         pltpu.VMEM((batch_rows, 2 * columns), bf16),
-        pltpu.VMEM((depths - 1, batch_rows, 2 * columns), bf16),
         pltpu.VMEM((2 * FRAME, FRAME), jnp.float32),
         pltpu.VMEM((FRAME, 2 * FRAME), bf16),
         dma((3,)),
@@ -921,12 +939,18 @@
         dma((angle_devs, kinds, slots)),
     ]
     scaling = 1.0 / (shear.shape[0] * angle_devs)
-    result, *_ = pl.pallas_call(
+    whole = (layers, 2, share, columns)
+    flushes = 2 - layers % 2
+    sums, picks, placed, *_ = pl.pallas_call(
         functools.partial(kernel, sizes, scaling),
-        out_shape=(jax.ShapeDtypeStruct((layers, 2, share, columns), jnp.float32),)
+        out_shape=(
+            jax.ShapeDtypeStruct(whole, jnp.float32),
+            jax.ShapeDtypeStruct((depths - 1, layers * share, batch_rows), bf16),
+            jax.ShapeDtypeStruct((depths - 1, batch_rows, 2 * columns), bf16),
+        )
         + tuple(jax.ShapeDtypeStruct(x, jnp.int32) for x in gathered),
         in_specs=[hbm] * 10,
-        out_specs=(vmem,) + (hbm,) * 2,
+        out_specs=(vmem,) * 3 + (hbm,) * 2,
         scratch_shapes=scratch,
         compiler_params=pltpu.CompilerParams(
             collective_id=0, has_side_effects=True, vmem_limit_bytes=VMEM_LIMIT
@@ -937,7 +961,14 @@
             for x in (crystal, probe, amplitude, dft, *small)
         )
     )
-    return result
+    return pl.pallas_call(
+        functools.partial(finish_kernel, flushes, scaling),
+        out_shape=jax.ShapeDtypeStruct(whole, jnp.float32),
+        in_specs=[vmem] * 3,
+        out_specs=hbm,
+        scratch_shapes=[pltpu.VMEM(whole, jnp.float32), dma((flushes,))],
+        compiler_params=pltpu.CompilerParams(vmem_limit_bytes=VMEM_LIMIT),
+    )(sums, picks, placed)
 
 
 def solution(mesh):

time: 17.6 us -> 17.6 us (level)
  local copies, waits for them, and re-layouts: 0.88 us -> 0 us
  Pallas kernels: 16.5 us -> 17.3 us
    pallas_call x0 -> x1, Pallas kernels: none -> 1.13 us  [body(): pl.pallas_call(functools.partial(finish_kernel, flushes, scaling), out_sh...]
    unnamed x1 -> x0, local copies, waits for them, and re-layouts: 0.88 us -> none
    pallas_call x1, Pallas kernels: 16.5 us -> 16.2 us  [body(): pl.pallas_call(functools.partial(kernel, sizes, scaling), out_shape=(jax....]
where the time goes in v7:
time: 17.6 us; the launch traced here: 17.3 us
  Pallas kernels  17.3 us (98%)
    pallas_call x1, Pallas kernels, body(): pl.pallas_call(functools.partial(kernel, sizes, scaling), out_shape=(jax....  16.2 us
    pallas_call x1, Pallas kernels, body(): pl.pallas_call(functools.partial(finish_kernel, flushes, scaling), out_sh...  1.13 us

profile of v7, /device:TPU:9, one launch (start us, length us, event | category | flops | bytes accessed | tf_op | source)
XLA Modules:
  0.0 17.3 jit_solution(991907568614979127)
XLA Ops:
  0.0 16.2 %shard_map.100 = (f32[4,2,64,384]{3,2,1,0:T(8,128)S(1)}, bf16[1,256,256]{2,1,0:T(8,128)(2,1)S(1)}, bf16[1,256,768]{2,1,0:T(8,128)(2,1)S(1)}, s32[2,4,4]{2,1,0:T(4,128)}, s32[2,3,1,2,4]{4,3,2,1,0:T(2,128)}) custom-call(bf16[4,2,128,384]{3,2,1,0:T(8,128)(2,1)} %crystal.1, bf16[2,256,256]{2,1,0:T(8,128)(2,1)} %probe_in.1, bf16[2,128,256]{2,1,0:T(8,128)(2,1)} %amplitude.1, ...), custom_call_target="tpu_custom_call" | custom-call | tf_op jit(solution)/shard_map/pallas_call | solution.py:944
  16.2 1.1 %shard_map.101 = f32[4,2,64,384]{3,2,1,0:T(8,128)} custom-call(f32[4,2,64,384]{3,2,1,0:T(8,128)S(1)} %get-tuple-element.8.sums, bf16[1,256,256]{2,1,0:T(8,128)(2,1)S(1)} %get-tuple-element.9.picks, bf16[1,256,768]{2,1,0:T(8,128)(2,1)S(1)} %get-tuple-element.10.placed), custom_call_target="tpu_custom_call" | custom-call | tf_op jit(solution)/shard_map/pallas_call | solution.py:964
